TPU v7x, 128 devices: a whole 4x4x4 slice. The times are simulated.
128 devices in a mesh: grp: 8 (over y, core), tm: 16 (over x, z).
Axes of the slice: x: 4, y: 4, z: 4, core: 2. Of those that a mesh axis runs over, the one named last changes fastest.
Arguments:
- raw: float32 [8192, 4096], P('grp', 'tm')
- channel_order: int32 [8, 1024], P('grp'), may hold values from 0 to 1023, each once within a row
- tile_list: int32 [255, 2], replicated, may hold values from 0 to 127, as said below
- tile_owner: int32 [255], replicated, may hold values from 0 to 127, as said below
Outputs:
- correlations: bfloat16 [256, 64, 64, 128], P(('grp', 'tm'))
Inputs may be any that keep to these rules, and one draw needn't show every extreme that they name: Each row of channel_order is a permutation of 0 .. 1023. `tile_list`: the rows are the tiles (b, b) for every block b and (b, b + 1) for every b < 127, each once, in a drawn order. `tile_owner`: the owner of a tile (b, b + 1) is b; the owner of a tile (b, b) is b + 1 for b < 127, and the last block's diagonal tile is owned by 128 - 1; no owner holds more than 2 tiles, and owner 128 - 1 holds exactly 2.
All inputs are finite; a program needn't handle non-finite values.
Results may differ from a plain program's by a relative error of at most 0.013.
Values may be sent and summed in bfloat16 or wider, within the bound.
No kernel may reach another device: no remote copies, remote signals or barrier semaphores. Data moves between devices by JAX's collectives and lax.ppermute only.
A program may use at most 64 MiB of HBM per device.

v0:
```python
import math

import jax
import jax.numpy as jnp
import numpy as np
from jax import lax
from jax.experimental import pallas as pl
from jax.experimental.pallas import tpu as pltpu
from jax.sharding import PartitionSpec as P

SEG_LEN = 256
BAND = 64
BAND_LO = 3
LAGS = 128
NORM_HALF = 64
TILE_CAP = 2
BLOCK = 64
SEGS = 16
HALF = BAND // 2
ROWS = SEGS * BLOCK
F32 = jnp.float32
BF16 = jnp.bfloat16


def split_bf16(values):
    high = values.astype(jnp.bfloat16)
    low = (values.astype(np.float32) - high.astype(np.float32)).astype(jnp.bfloat16)
    return high, low


def band_table():
    source = np.arange(2 * SEG_LEN) - SEG_LEN // 2
    target = np.arange(SEG_LEN)
    return (np.abs(source[:, None] - target[None, :]) <= NORM_HALF).astype(jnp.bfloat16)


def frequency_rows():
    row = np.arange(2 * BAND)
    upper, part, place = row // BAND, (row // HALF) % 2, row % HALF
    return upper * HALF + place, part


def dft_table():
    freq, part = frequency_rows()
    sample = np.arange(SEG_LEN)
    angle = ((freq[:, None] + BAND_LO) * sample[None, :] % SEG_LEN) * (2.0 * math.pi / SEG_LEN)
    table = np.where(part[:, None] == 0, np.cos(angle), -np.sin(angle)).astype(np.float32)
    return np.concatenate(split_bf16(table), axis=0)


def smooth_tables():
    freq, _ = frequency_rows()
    weights = (BAND - np.abs(freq[:, None] - freq[None, :])).astype(np.float32)
    band = np.arange(BAND)
    total = (BAND - np.abs(band[:, None] - band[None, :])).sum(axis=0).astype(np.float32)
    taper = 0.5 - 0.5 * np.cos((freq + 0.5) * (2.0 * math.pi / BAND))
    shape = (2 * BAND, 2 * BLOCK)
    scale = np.stack(
        [
            np.broadcast_to((1.0 / total[freq])[:, None], shape),
            np.broadcast_to(taper[:, None], shape),
        ]
    ).astype(np.float32)
    return np.concatenate([weights, weights], axis=1).astype(jnp.bfloat16), scale


def lag_table():
    row = np.arange(2 * BAND)
    upper, place, part = row // BAND, (row // 2) % HALF, row % 2
    freq = upper * HALF + place + BAND_LO
    lag = np.arange(LAGS) - LAGS // 2
    angle = (freq[:, None] * lag[None, :] % SEG_LEN) * (2.0 * math.pi / SEG_LEN)
    table = np.where(part[:, None] == 0, np.cos(angle), -np.sin(angle))
    table = table.astype(np.float32).astype(jnp.bfloat16).astype(np.float32)
    return (table / math.sqrt(SEGS * BAND)).astype(jnp.bfloat16)


def dot(left, right, left_dim=1, right_dim=0):
    return lax.dot_general(
        left, right, (((left_dim,), (right_dim,)), ((), ())), preferred_element_type=F32
    )


def low_lanes(shape):
    return lax.broadcasted_iota(jnp.int32, shape, 1) < BLOCK


def sort_kernel(order_ref, raw_ref, out_ref, raw_low):
    channels = raw_ref.shape[0]
    raw_low[...] = raw_ref[...].astype(BF16)
    lanes = lax.broadcasted_iota(jnp.int32, (128, 128), 1)
    for chunk in range(channels // 128):
        wanted = jnp.broadcast_to(order_ref[chunk : chunk + 1, :], (128, 128)).T
        pieces = [
            jnp.where(wanted == lanes + 128 * piece, 1.0, 0.0).astype(BF16)
            for piece in range(channels // 128)
        ]
        picked = dot(jnp.concatenate(pieces, axis=1), raw_low[...])
        out_ref[pl.ds(chunk * 128, 128), :] = picked.astype(BF16)


def sort_rows(raw, order):
    channels, samples = raw.shape
    return pl.pallas_call(
        sort_kernel,
        out_shape=jax.ShapeDtypeStruct((channels, samples), BF16),
        in_specs=[pl.BlockSpec(memory_space=pltpu.VMEM)] * 2,
        out_specs=pl.BlockSpec(memory_space=pltpu.VMEM),
        scratch_shapes=[pltpu.VMEM((channels, samples), BF16)],
        name="sort_rows",
    )(order.reshape(channels // 128, 128), raw)


def whiten_kernel(x_ref, band_ref, dft_ref, smooth_ref, scale_ref, out_ref, held):
    low = low_lanes((BAND, 2 * BLOCK))
    half_seg = SEG_LEN // 2
    for pair in range(SEGS // 2):
        start = pair * 2 * BLOCK
        x = x_ref[start : start + 2 * BLOCK, :].astype(F32)
        size = jnp.abs(x)
        blank = jnp.zeros((BLOCK, half_seg), F32)
        before = (
            jnp.abs(x_ref[start - BLOCK : start, half_seg:].astype(F32)) if pair > 0 else blank
        )
        stop = start + 2 * BLOCK
        after = (
            jnp.abs(x_ref[stop : stop + BLOCK, :half_seg].astype(F32))
            if pair < SEGS // 2 - 1
            else blank
        )
        before = jnp.concatenate([before, size[:BLOCK, half_seg:]], axis=0)
        after = jnp.concatenate([size[BLOCK:, :half_seg], after], axis=0)
        around = jnp.concatenate([before, size, after], axis=1).astype(BF16)
        mean = dot(around, band_ref[...]) * (1.0 / (2 * NORM_HALF + 1))
        normed = x / (mean + 1e-05)
        normed_high = normed.astype(BF16)
        normed_low = (normed - normed_high.astype(F32)).astype(BF16)
        both = dot(dft_ref[...], normed_high, 1, 1)
        spectrum = (both[: 2 * BAND] + both[2 * BAND :]) + dot(
            dft_ref[: 2 * BAND, :], normed_low, 1, 1
        )
        power = spectrum * spectrum
        power_high = power.astype(BF16)
        power_low = (power - power_high.astype(F32)).astype(BF16)
        smoothed = dot(smooth_ref[...], jnp.concatenate([power_high, power_low], axis=0))
        white = spectrum * (scale_ref[1] / jnp.sqrt(smoothed * scale_ref[0] + 1e-06))
        lower, upper = white[:BAND], white[BAND:]
        turned = pltpu.roll(jnp.where(low, upper, lower), BLOCK, 1)
        first = jnp.where(low, lower, turned)
        second = jnp.where(low, turned, upper)
        for segment, value in ((2 * pair, first), (2 * pair + 1, second)):
            for part in range(2):
                held[pl.ds(part * SEGS + segment, HALF, stride=2 * SEGS), :] = value[
                    part * HALF : (part + 1) * HALF
                ]
    out_ref[...] = held[...].astype(BF16)


def whiten(x):
    band, dft = band_table(), dft_table()
    smooth, scale = smooth_tables()
    return pl.pallas_call(
        whiten_kernel,
        out_shape=jax.ShapeDtypeStruct((ROWS, 2 * BLOCK), BF16),
        in_specs=[pl.BlockSpec(memory_space=pltpu.VMEM)] * 5,
        out_specs=pl.BlockSpec(memory_space=pltpu.VMEM),
        scratch_shapes=[pltpu.VMEM((ROWS, 2 * BLOCK), F32)],
        name="whiten",
    )(x, band, dft, smooth, scale)


def fill_cross(left_ref, right_ref, cross, left_twice=False):
    low = low_lanes((2 * SEGS, 2 * BLOCK))
    for place in range(HALF):
        start = place * 2 * SEGS
        left = left_ref[start : start + 2 * SEGS, :].astype(F32)
        right = right_ref[start : start + 2 * SEGS, :].astype(F32)
        right = jnp.where(left_twice, left, right)
        other = jnp.concatenate([left[SEGS:], -left[:SEGS]], axis=0)
        turned = pltpu.roll(jnp.where(low, other, left), BLOCK, 1)
        rows = jnp.concatenate(
            [jnp.where(low, left, turned), jnp.where(low, turned, other)], axis=0
        ).astype(BF16)
        columns = jnp.concatenate(
            [jnp.where(low, right, 0.0), jnp.where(low, 0.0, right)], axis=0
        ).astype(BF16)
        cross[place * 2 * BLOCK : (place + 1) * 2 * BLOCK, :] = dot(rows, columns, 0, 0)


def tile_kernel(tiles_ref, own_ref, before_ref, after_ref, lag_ref, out_ref, cross, stage, sem):
    own = lax.axis_index("grp") * lax.axis_size("tm") + lax.axis_index("tm")
    last = lax.axis_size("grp") * lax.axis_size("tm") - 1
    tiles = tiles_ref[...]
    position = lax.broadcasted_iota(jnp.int32, (tiles.shape[0], 1), 0)

    def place_of(first, second):
        found = (tiles[:, 0:1] == first) & (tiles[:, 1:2] == second)
        return jnp.sum(jnp.where(found, position, 0))

    diagonal = place_of(own - 1, own - 1)
    other = place_of(own, jnp.minimum(own + 1, last))
    diagonal_first = (own > 0) & (diagonal < other)
    low = low_lanes((2 * HALF, 2 * BLOCK))

    def lags(number, slot):
        for pair in range(BLOCK // 2):
            first = cross[pl.ds(2 * pair, 2 * HALF, stride=BLOCK), :]
            second = cross[pl.ds(2 * pair + 1, 2 * HALF, stride=BLOCK), :]
            turned = pltpu.roll(jnp.where(low, second, first), BLOCK, 1)
            both = jnp.concatenate(
                [jnp.where(low, first, turned), jnp.where(low, turned, second)], axis=0
            ).astype(BF16)
            stage[number, 2 * pair * BLOCK : 2 * (pair + 1) * BLOCK, :] = dot(
                both, lag_ref[...], 0, 0
            ).astype(BF16)
        pltpu.make_async_copy(stage.at[number], out_ref.at[slot], sem.at[number]).start()

    first_slot = jnp.where(diagonal_first, 0, 1)
    fill_cross(before_ref, before_ref, cross)
    lags(0, first_slot)
    fill_cross(own_ref, after_ref, cross, own == last)
    lags(1, 1 - first_slot)
    pltpu.make_async_copy(stage.at[0], out_ref.at[first_slot], sem.at[0]).wait()
    pltpu.make_async_copy(stage.at[1], out_ref.at[1 - first_slot], sem.at[1]).wait()


def correlate(tiles, own, before, after):
    vmem = pl.BlockSpec(memory_space=pltpu.VMEM)
    return pl.pallas_call(
        tile_kernel,
        out_shape=jax.ShapeDtypeStruct((TILE_CAP, BLOCK * BLOCK, LAGS), BF16),
        in_specs=[vmem] * 5,
        out_specs=pl.BlockSpec(memory_space=pl.ANY),
        scratch_shapes=[
            pltpu.VMEM((HALF * 2 * BLOCK, 2 * BLOCK), F32),
            pltpu.VMEM((TILE_CAP, BLOCK * BLOCK, LAGS), BF16),
            pltpu.SemaphoreType.DMA((TILE_CAP,)),
        ],
        name="correlate",
    )(tiles, own, before, after, lag_table())


def per_device(raw, channel_order, tile_list, tile_owner):
    count = lax.axis_size("grp") * lax.axis_size("tm")
    ordered = sort_rows(raw, channel_order[0])
    parts = ordered.reshape(SEGS, BLOCK, SEG_LEN)
    record = lax.all_to_all(parts, "tm", split_axis=0, concat_axis=0, tiled=True)
    own = whiten(record.reshape(ROWS, SEG_LEN))
    up = [(i, i + 1) for i in range(count - 1)]
    down = [(i + 1, i) for i in range(count - 1)]
    before = lax.ppermute(own, ("grp", "tm"), up)
    after = lax.ppermute(own, ("grp", "tm"), down)
    out = correlate(tile_list, own, before, after)
    return out.reshape(TILE_CAP, BLOCK, BLOCK, LAGS)


def solution(mesh):
    return jax.shard_map(
        per_device,
        mesh=mesh,
        in_specs=(P("grp", "tm"), P("grp", None), P(), P()),
        out_specs=P(("grp", "tm"), None, None, None),
        check_vma=False,
    )
```

profile of v0, /device:TPU:1, one launch (start us, length us, event | category | flops | bytes accessed | tf_op | source)
XLA Modules:
  0.0 54.0 jit_solution(14053690336320344330)
XLA Ops:
  0.0 0.0 copy-start.2
  0.0 2.8 %sort_rows.1 = bf16[1024,256]{1,0:T(8,128)(2,1)} custom-call(s32[8,128]{1,0:T(8,128)} %bitcast.6, f32[1024,256]{1,0:T(8,128)} %raw_ref.1), custom_call_target="tpu_custom_call" | custom-call | tf_op jit(solution)/shard_map/sort_rows/pallas_call | solution.py:104
  2.9 18.8 %all_to_all.5 = bf16[16,64,256]{2,1,0:T(8,128)(2,1)} all-to-all(bf16[16,64,256]{2,1,0:T(8,128)(2,1)} %bitcast.4), channel_id=1, replica_groups=mesh['grp'=8,'tm'=16] {'tm'}, dimensions={0} | all-to-all | bytes 1048576 | tf_op jit(solution)/shard_map/all_to_all | solution.py:247
  21.7 6.0 %whiten.1.own_ref = bf16[1024,128]{1,0:T(8,128)(2,1)} custom-call(bf16[1024,256]{1,0:T(8,128)(2,1)} %bitcast.5, bf16[512,256]{1,0:T(8,128)(2,1)} %constant.10.clone.band_ref, bf16[256,256]{1,0:T(8,128)(2,1)} %constant.11.clone.dft_ref, bf16[128,256]{1,0:T(8,128)(2,1)} %constant.12.clone.smooth_ref, f32[2,128,128]{2,1,0:T(8,128)} %constant.13.clone.scale_ref), custom_call_target="tpu_custom_call" | custom-call | tf_op jit(solution)/shard_map/whiten/pallas_call | solution.py:162
  27.6 4.8 %collective-permute-start.1 = (bf16[1024,128]{1,0:T(8,128)(2,1)}, bf16[1024,128]{1,0:T(8,128)(2,1)S(1)}, u32[]{:S(2)}, u32[]{:S(2)}) collective-permute-start(bf16[1024,128]{1,0:T(8,128)(2,1)} %whiten.1.own_ref), channel_id=1, source_target_pairs={{1,0},{2,1},{3,2},{4,3},{5,4},{6,5},{7,6},{8,7},{9,8},{10,9},{11,1... | collective-permute-start | bytes 786440 | tf_op jit(solution)/shard_map/ppermute | solution.py:252
  32.5 1.9 %collective-permute-start = (bf16[1024,128]{1,0:T(8,128)(2,1)}, bf16[1024,128]{1,0:T(8,128)(2,1)S(1)}, u32[]{:S(2)}, u32[]{:S(2)}) collective-permute-start(bf16[1024,128]{1,0:T(8,128)(2,1)} %whiten.1.own_ref), channel_id=1, source_target_pairs={{0,1},{1,2},{2,3},{3,4},{4,5},{5,6},{6,7},{7,8},{8,9},{9,10},{10,1... | collective-permute-start | bytes 786440 | tf_op jit(solution)/shard_map/ppermute | solution.py:251
  34.4 0.0 copy-done.2
  34.4 0.8 %copy.9.tiles_ref = s32[255,2]{1,0:T(8,128)} copy(s32[255,2]{0,1:T(2,128)S(1)} %copy-done.2) | data formatting | bytes 4080 | tf_op args[2]
  35.2 1.0 %collective-permute-done.1.after_ref = bf16[1024,128]{1,0:T(8,128)(2,1)S(1)} collective-permute-done((bf16[1024,128]{1,0:T(8,128)(2,1)}, bf16[1024,128]{1,0:T(8,128)(2,1)S(1)}, u32[]{:S(2)}, u32[]{:S(2)}) %collective-permute-start.1) | collective-permute-done | bytes 262176 | tf_op jit(solution)/shard_map/ppermute | solution.py:252
  36.2 0.0 copy-start
  36.2 9.8 %collective-permute-done.before_ref = bf16[1024,128]{1,0:T(8,128)(2,1)S(1)} collective-permute-done((bf16[1024,128]{1,0:T(8,128)(2,1)}, bf16[1024,128]{1,0:T(8,128)(2,1)S(1)}, u32[]{:S(2)}, u32[]{:S(2)}) %collective-permute-start) | collective-permute-done | bytes 262176 | tf_op jit(solution)/shard_map/ppermute | solution.py:251
  46.1 0.0 copy-done
  46.1 0.0 copy-start.1
  46.1 0.7 %copy-done.1 = bf16[1024,128]{1,0:T(8,128)(2,1)} copy-done((bf16[1024,128]{1,0:T(8,128)(2,1)}, bf16[1024,128]{1,0:T(8,128)(2,1)S(1)}, u32[]{:S(2)}) %copy-start.1) | copy-done | bytes 262168
  46.8 7.3 %correlate.1 = bf16[2,4096,128]{2,1,0:T(8,128)(2,1)} custom-call(s32[255,2]{1,0:T(8,128)} %copy.9.tiles_ref, bf16[1024,128]{1,0:T(8,128)(2,1)} %whiten.1.own_ref, bf16[1024,128]{1,0:T(8,128)(2,1)} %copy-done.1, bf16[1024,128]{1,0:T(8,128)(2,1)} %copy-done, bf16[128,128]{1,0:T(8,128)(2,1)} %constant.14.clone.lag_ref), custom_call_target="tpu_custom_call" | custom-call | tf_op jit(solution)/shard_map/correlate/pallas_call | solution.py:229
Async XLA Ops:
  0.0 34.4 %copy-start.2 = (s32[255,2]{0,1:T(2,128)S(1)}, s32[255,2]{0,1:T(2,128)}, u32[]{:S(2)}) copy-start(s32[255,2]{0,1:T(2,128)} %param.11) | copy-start | bytes 6124
  27.6 8.6 %collective-permute-start.1 = (bf16[1024,128]{1,0:T(8,128)(2,1)}, bf16[1024,128]{1,0:T(8,128)(2,1)S(1)}, u32[]{:S(2)}, u32[]{:S(2)}) collective-permute-start(bf16[1024,128]{1,0:T(8,128)(2,1)} %whiten.1.own_ref), channel_id=1, source_target_pairs={{1,0},{2,1},{3,2},{4,3},{5,4},{6,5},{7,6},{8,7},{9,8},{10,9},{11,1... | collective-permute-start | bytes 786440 | tf_op jit(solution)/shard_map/ppermute | solution.py:252
  32.5 13.6 %collective-permute-start = (bf16[1024,128]{1,0:T(8,128)(2,1)}, bf16[1024,128]{1,0:T(8,128)(2,1)S(1)}, u32[]{:S(2)}, u32[]{:S(2)}) collective-permute-start(bf16[1024,128]{1,0:T(8,128)(2,1)} %whiten.1.own_ref), channel_id=1, source_target_pairs={{0,1},{1,2},{2,3},{3,4},{4,5},{5,6},{6,7},{7,8},{8,9},{9,10},{10,1... | collective-permute-start | bytes 786440 | tf_op jit(solution)/shard_map/ppermute | solution.py:251
  36.2 9.8 %copy-start = (bf16[1024,128]{1,0:T(8,128)(2,1)}, bf16[1024,128]{1,0:T(8,128)(2,1)S(1)}, u32[]{:S(2)}) copy-start(bf16[1024,128]{1,0:T(8,128)(2,1)S(1)} %collective-permute-done.1.after_ref) | copy-start | bytes 786436
  46.1 0.7 %copy-start.1 = (bf16[1024,128]{1,0:T(8,128)(2,1)}, bf16[1024,128]{1,0:T(8,128)(2,1)S(1)}, u32[]{:S(2)}) copy-start(bf16[1024,128]{1,0:T(8,128)(2,1)S(1)} %collective-permute-done.before_ref) | copy-start | bytes 786436
where the time goes:
time: 54.4 us; the launch traced here: 54 us
  blocking collectives  18.8 us (35%)
  Pallas kernels  16.1 us (30%)
  waiting for transfers between devices  10.9 us (20%)
  starting transfers between devices  6.74 us (12%)
  local copies, waits for them, and re-layouts  1.49 us (3%)
    all_to_all x1, blocking collectives, per_device(): lax.all_to_all(parts, 'tm', split_axis=0, concat_axis=0, tiled=True)  18.8 us
    ppermute x1, waiting for transfers between devices, per_device(): before = lax.ppermute(own, ('grp', 'tm'), up)  9.82 us
    pallas_call x1, Pallas kernels, correlate(): pl.pallas_call(tile_kernel, out_shape=jax.ShapeDtypeStruct((TILE_CAP, BLO...  7.29 us
    pallas_call x1, Pallas kernels, whiten(): pl.pallas_call(whiten_kernel, out_shape=jax.ShapeDtypeStruct((ROWS, 2 * B...  5.97 us
    ppermute x1, starting transfers between devices, per_device(): after = lax.ppermute(own, ('grp', 'tm'), down)  4.82 us
    pallas_call x1, Pallas kernels, sort_rows(): pl.pallas_call(sort_kernel, out_shape=jax.ShapeDtypeStruct((channels, sam...  2.85 us
    ppermute x1, starting transfers between devices, per_device(): before = lax.ppermute(own, ('grp', 'tm'), up)  1.92 us
    unnamed x7, local copies, waits for them, and re-layouts  1.49 us
  transfers between devices with their start and end apart: 2, of which 2 were waited for; matrix products, arithmetic and copies ran while one was open for 1% of the time, Pallas kernels for 0%

commit v1 on v0

--- a/solution.py
+++ b/solution.py
@@ -169,75 +169,88 @@
     )(x, band, dft, smooth, scale)
 
 
-def fill_cross(left_ref, right_ref, cross, left_twice=False):
+def fill_cross(left_at, right_at, cross):
     low = low_lanes((2 * SEGS, 2 * BLOCK))
     for place in range(HALF):
-        start = place * 2 * SEGS
-        left = left_ref[start : start + 2 * SEGS, :].astype(F32)
-        right = right_ref[start : start + 2 * SEGS, :].astype(F32)
-        right = jnp.where(left_twice, left, right)
+        rows = pl.ds(place * 2 * SEGS, 2 * SEGS)
+        left = left_at(rows).astype(F32)
+        right = right_at(rows).astype(F32)
         other = jnp.concatenate([left[SEGS:], -left[:SEGS]], axis=0)
         turned = pltpu.roll(jnp.where(low, other, left), BLOCK, 1)
-        rows = jnp.concatenate(
+        left = jnp.concatenate(
             [jnp.where(low, left, turned), jnp.where(low, turned, other)], axis=0
         ).astype(BF16)
-        columns = jnp.concatenate(
+        right = jnp.concatenate(
             [jnp.where(low, right, 0.0), jnp.where(low, 0.0, right)], axis=0
         ).astype(BF16)
-        cross[place * 2 * BLOCK : (place + 1) * 2 * BLOCK, :] = dot(rows, columns, 0, 0)
-
-
-def tile_kernel(tiles_ref, own_ref, before_ref, after_ref, lag_ref, out_ref, cross, stage, sem):
+        cross[place * 2 * BLOCK : (place + 1) * 2 * BLOCK, :] = dot(left, right, 0, 0)
+
+
+def fill_lags(cross, lag_ref, stage):
+    low = low_lanes((2 * HALF, 2 * BLOCK))
+    for pair in range(BLOCK // 2):
+        first = cross[pl.ds(2 * pair, 2 * HALF, stride=BLOCK), :]
+        second = cross[pl.ds(2 * pair + 1, 2 * HALF, stride=BLOCK), :]
+        turned = pltpu.roll(jnp.where(low, second, first), BLOCK, 1)
+        both = jnp.concatenate(
+            [jnp.where(low, first, turned), jnp.where(low, turned, second)], axis=0
+        ).astype(BF16)
+        rows = slice(2 * pair * BLOCK, 2 * (pair + 1) * BLOCK)
+        stage[rows, :] = dot(both, lag_ref[...], 0, 0).astype(BF16)
+
+
+def diagonal_slot(tiles_ref, own, last):
+    position = lax.broadcasted_iota(jnp.int32, (1, tiles_ref.shape[1]), 1)
+
+    def place_of(first, second):
+        found = (tiles_ref[0:1, :] == first) & (tiles_ref[1:2, :] == second)
+        return jnp.sum(jnp.where(found, position, 0))
+
+    diagonal = place_of(own - 1, own - 1)
+    other = place_of(own, jnp.minimum(own + 1, last))
+    return jnp.where((own > 0) & (diagonal < other), 0, 1)
+
+
+def tile_kernel(swap, tiles_ref, own_ref, other_ref, lag_ref, *rest):
+    out_ref, cross, stage, sem = rest[-4:]
     own = lax.axis_index("grp") * lax.axis_size("tm") + lax.axis_index("tm")
     last = lax.axis_size("grp") * lax.axis_size("tm") - 1
-    tiles = tiles_ref[...]
-    position = lax.broadcasted_iota(jnp.int32, (tiles.shape[0], 1), 0)
-
-    def place_of(first, second):
-        found = (tiles[:, 0:1] == first) & (tiles[:, 1:2] == second)
-        return jnp.sum(jnp.where(found, position, 0))
-
-    diagonal = place_of(own - 1, own - 1)
-    other = place_of(own, jnp.minimum(own + 1, last))
-    diagonal_first = (own > 0) & (diagonal < other)
-    low = low_lanes((2 * HALF, 2 * BLOCK))
-
-    def lags(number, slot):
-        for pair in range(BLOCK // 2):
-            first = cross[pl.ds(2 * pair, 2 * HALF, stride=BLOCK), :]
-            second = cross[pl.ds(2 * pair + 1, 2 * HALF, stride=BLOCK), :]
-            turned = pltpu.roll(jnp.where(low, second, first), BLOCK, 1)
-            both = jnp.concatenate(
-                [jnp.where(low, first, turned), jnp.where(low, turned, second)], axis=0
-            ).astype(BF16)
-            stage[number, 2 * pair * BLOCK : 2 * (pair + 1) * BLOCK, :] = dot(
-                both, lag_ref[...], 0, 0
-            ).astype(BF16)
-        pltpu.make_async_copy(stage.at[number], out_ref.at[slot], sem.at[number]).start()
-
-    first_slot = jnp.where(diagonal_first, 0, 1)
-    fill_cross(before_ref, before_ref, cross)
-    lags(0, first_slot)
-    fill_cross(own_ref, after_ref, cross, own == last)
-    lags(1, 1 - first_slot)
-    pltpu.make_async_copy(stage.at[0], out_ref.at[first_slot], sem.at[0]).wait()
-    pltpu.make_async_copy(stage.at[1], out_ref.at[1 - first_slot], sem.at[1]).wait()
-
-
-def correlate(tiles, own, before, after):
+    is_diagonal = own % 2 == (1 if swap == 0 else 0)
+    no_other = (own == last) if swap == 1 else False
+
+    def left_at(rows):
+        return jnp.where(is_diagonal, other_ref[rows, :].astype(F32), own_ref[rows, :].astype(F32))
+
+    def right_at(rows):
+        if swap == 0:
+            return other_ref[rows, :]
+        return jnp.where(no_other, own_ref[rows, :].astype(F32), other_ref[rows, :].astype(F32))
+
+    fill_cross(left_at, right_at, cross)
+    fill_lags(cross, lag_ref, stage)
+    slot = diagonal_slot(tiles_ref, own, last)
+    slot = jnp.where(is_diagonal, slot, 1 - slot)
+    copy = pltpu.make_async_copy(stage, out_ref.at[slot], sem)
+    copy.start()
+    copy.wait()
+
+
+def correlate(swap, tiles, own, other, held=()):
     vmem = pl.BlockSpec(memory_space=pltpu.VMEM)
+    anywhere = pl.BlockSpec(memory_space=pl.ANY)
     return pl.pallas_call(
-        tile_kernel,
+        lambda *refs: tile_kernel(swap, *refs),
         out_shape=jax.ShapeDtypeStruct((TILE_CAP, BLOCK * BLOCK, LAGS), BF16),
-        in_specs=[vmem] * 5,
-        out_specs=pl.BlockSpec(memory_space=pl.ANY),
+        in_specs=[vmem] * 4 + [anywhere] * len(held),
+        out_specs=anywhere,
         scratch_shapes=[
             pltpu.VMEM((HALF * 2 * BLOCK, 2 * BLOCK), F32),
-            pltpu.VMEM((TILE_CAP, BLOCK * BLOCK, LAGS), BF16),
-            pltpu.SemaphoreType.DMA((TILE_CAP,)),
+            pltpu.VMEM((BLOCK * BLOCK, LAGS), BF16),
+            pltpu.SemaphoreType.DMA,
         ],
-        name="correlate",
-    )(tiles, own, before, after, lag_table())
+        input_output_aliases={4: 0} if held else {},
+        name=f"correlate_{swap}",
+    )(tiles, own, other, lag_table(), *held)
 
 
 def per_device(raw, channel_order, tile_list, tile_owner):
@@ -246,11 +259,13 @@
     parts = ordered.reshape(SEGS, BLOCK, SEG_LEN)
     record = lax.all_to_all(parts, "tm", split_axis=0, concat_axis=0, tiled=True)
     own = whiten(record.reshape(ROWS, SEG_LEN))
-    up = [(i, i + 1) for i in range(count - 1)]
-    down = [(i + 1, i) for i in range(count - 1)]
-    before = lax.ppermute(own, ("grp", "tm"), up)
-    after = lax.ppermute(own, ("grp", "tm"), down)
-    out = correlate(tile_list, own, before, after)
+    pairs = [(i, i ^ 1) for i in range(count)]
+    shifted = [(i, i + 1 if i % 2 else i - 1) for i in range(1, count - 1)]
+    near = lax.ppermute(own, ("grp", "tm"), pairs)
+    far = lax.ppermute(own, ("grp", "tm"), shifted)
+    tiles = tile_list.T
+    out = correlate(0, tiles, own, near)
+    out = correlate(1, tiles, own, far, (out,))
     return out.reshape(TILE_CAP, BLOCK, BLOCK, LAGS)
 
 

time: 54.4 us -> 47.1 us (0.87)
  the two profiles are of different devices: /device:TPU:1 before, /device:TPU:24 now
where the time goes in v1:
time: 47.1 us; the launch traced here: 46.8 us
  blocking collectives  19.5 us (41%)
  Pallas kernels  17.9 us (38%)
  waiting for transfers between devices  5.53 us (12%)
  starting transfers between devices  2.47 us (5%)
  local copies, waits for them, and re-layouts  1.38 us (3%)
    all_to_all x1, blocking collectives, per_device(): lax.all_to_all(parts, 'tm', split_axis=0, concat_axis=0, tiled=True)  19.5 us
    pallas_call x2, Pallas kernels, correlate(): pl.pallas_call(lambda *refs: tile_kernel(swap, *refs), out_shape=jax.Shap...  9.1 us
    pallas_call x1, Pallas kernels, whiten(): pl.pallas_call(whiten_kernel, out_shape=jax.ShapeDtypeStruct((ROWS, 2 * B...  5.97 us
    ppermute x1, waiting for transfers between devices, per_device(): near = lax.ppermute(own, ('grp', 'tm'), pairs)  4.31 us
    pallas_call x1, Pallas kernels, sort_rows(): pl.pallas_call(sort_kernel, out_shape=jax.ShapeDtypeStruct((channels, sam...  2.83 us
    ppermute x1, starting transfers between devices, per_device(): far = lax.ppermute(own, ('grp', 'tm'), shifted)  1.91 us
    unnamed x4, local copies, waits for them, and re-layouts  1.38 us
    ppermute x1, waiting for transfers between devices, per_device(): far = lax.ppermute(own, ('grp', 'tm'), shifted)  1.23 us
  transfers between devices with their start and end apart: 2, of which 2 were waited for; matrix products, arithmetic and copies ran while one was open for 0% of the time, Pallas kernels for 10%

profile of v1, /device:TPU:24, one launch (start us, length us, event | category | flops | bytes accessed | tf_op | source)
XLA Modules:
  0.0 46.8 jit_solution(14493037714839816315)
XLA Ops:
  0.0 2.8 %sort_rows.1 = bf16[1024,256]{1,0:T(8,128)(2,1)} custom-call(s32[8,128]{1,0:T(8,128)} %bitcast.9, f32[1024,256]{1,0:T(8,128)} %raw_ref.1), custom_call_target="tpu_custom_call" | custom-call | tf_op jit(solution)/shard_map/sort_rows/pallas_call | solution.py:104
  2.8 19.5 %all_to_all.5 = bf16[16,64,256]{2,1,0:T(8,128)(2,1)} all-to-all(bf16[16,64,256]{2,1,0:T(8,128)(2,1)} %bitcast.5), channel_id=1, replica_groups=mesh['grp'=8,'tm'=16] {'tm'}, dimensions={0} | all-to-all | bytes 1048576 | tf_op jit(solution)/shard_map/all_to_all | solution.py:260
  22.3 6.0 %whiten.1.refs_1_ = bf16[1024,128]{1,0:T(8,128)(2,1)} custom-call(bf16[1024,256]{1,0:T(8,128)(2,1)} %bitcast.6, bf16[512,256]{1,0:T(8,128)(2,1)} %constant.10.clone.band_ref, bf16[256,256]{1,0:T(8,128)(2,1)} %constant.11.clone.dft_ref, bf16[128,256]{1,0:T(8,128)(2,1)} %constant.12.clone.smooth_ref, f32[2,128,128]{2,1,0:T(8,128)} %constant.13.clone.scale_ref), custom_call_target="tpu_custom_call" | custom-call | tf_op jit(solution)/shard_map/whiten/pallas_call | solution.py:162
  28.3 0.6 %collective-permute-start.1 = (bf16[1024,128]{1,0:T(8,128)(2,1)}, bf16[1024,128]{1,0:T(8,128)(2,1)S(1)}, u32[]{:S(2)}, u32[]{:S(2)}) collective-permute-start(bf16[1024,128]{1,0:T(8,128)(2,1)} %whiten.1.refs_1_), channel_id=1, source_target_pairs={{0,1},{1,0},{2,3},{3,2},{4,5},{5,4},{6,7},{7,6},{8,9},{9,8},{10,11... | collective-permute-start | bytes 786440 | tf_op jit(solution)/shard_map/ppermute | solution.py:264
  28.8 1.9 %collective-permute-start = (bf16[1024,128]{1,0:T(8,128)(2,1)}, bf16[1024,128]{1,0:T(8,128)(2,1)S(1)}, u32[]{:S(2)}, u32[]{:S(2)}) collective-permute-start(bf16[1024,128]{1,0:T(8,128)(2,1)} %whiten.1.refs_1_), channel_id=1, source_target_pairs={{1,2},{2,1},{3,4},{4,3},{5,6},{6,5},{7,8},{8,7},{9,10},{10,9},{11,... | collective-permute-start | bytes 786440 | tf_op jit(solution)/shard_map/ppermute | solution.py:265
  30.7 4.3 %collective-permute-done.1.refs_2_ = bf16[1024,128]{1,0:T(8,128)(2,1)S(1)} collective-permute-done((bf16[1024,128]{1,0:T(8,128)(2,1)}, bf16[1024,128]{1,0:T(8,128)(2,1)S(1)}, u32[]{:S(2)}, u32[]{:S(2)}) %collective-permute-start.1) | collective-permute-done | bytes 262176 | tf_op jit(solution)/shard_map/ppermute | solution.py:264
  35.1 0.0 copy-start.1
  35.1 0.7 %copy-done.1 = bf16[1024,128]{1,0:T(8,128)(2,1)} copy-done((bf16[1024,128]{1,0:T(8,128)(2,1)}, bf16[1024,128]{1,0:T(8,128)(2,1)S(1)}, u32[]{:S(2)}) %copy-start.1) | copy-done | bytes 262168
  35.7 4.5 %correlate_0.1.refs_4_ = bf16[2,4096,128]{2,1,0:T(8,128)(2,1)} custom-call(s32[2,255]{1,0:T(2,128)} %bitcast.7, bf16[1024,128]{1,0:T(8,128)(2,1)} %whiten.1.refs_1_, bf16[1024,128]{1,0:T(8,128)(2,1)} %copy-done.1, bf16[128,128]{1,0:T(8,128)(2,1)} %constant.14.clone.refs_3_), custom_call_target="tpu_custom_call" | custom-call | tf_op jit(solution)/shard_map/correlate_0/pallas_call | solution.py:241
  40.3 1.2 %collective-permute-done.refs_2_ = bf16[1024,128]{1,0:T(8,128)(2,1)S(1)} collective-permute-done((bf16[1024,128]{1,0:T(8,128)(2,1)}, bf16[1024,128]{1,0:T(8,128)(2,1)S(1)}, u32[]{:S(2)}, u32[]{:S(2)}) %collective-permute-start) | collective-permute-done | bytes 262176 | tf_op jit(solution)/shard_map/ppermute | solution.py:265
  41.5 0.0 copy-start
  41.5 0.7 %copy-done = bf16[1024,128]{1,0:T(8,128)(2,1)} copy-done((bf16[1024,128]{1,0:T(8,128)(2,1)}, bf16[1024,128]{1,0:T(8,128)(2,1)S(1)}, u32[]{:S(2)}) %copy-start) | copy-done | bytes 262168
  42.2 4.6 %correlate_1.1 = bf16[2,4096,128]{2,1,0:T(8,128)(2,1)} custom-call(s32[2,255]{1,0:T(2,128)} %bitcast.8, bf16[1024,128]{1,0:T(8,128)(2,1)} %whiten.1.refs_1_, bf16[1024,128]{1,0:T(8,128)(2,1)} %copy-done, bf16[128,128]{1,0:T(8,128)(2,1)} %constant.14.clone.refs_3_, bf16[2,4096,128]{2,1,0:T(8,128)(2,1)} %correlate_0.1.refs_4_), custom_call_target="tpu_custom_call", output_to_operand_aliasing={{}: (4, {})} | custom-call | tf_op jit(solution)/shard_map/correlate_1/pallas_call | solution.py:241
Async XLA Ops:
  28.3 6.8 %collective-permute-start.1 = (bf16[1024,128]{1,0:T(8,128)(2,1)}, bf16[1024,128]{1,0:T(8,128)(2,1)S(1)}, u32[]{:S(2)}, u32[]{:S(2)}) collective-permute-start(bf16[1024,128]{1,0:T(8,128)(2,1)} %whiten.1.refs_1_), channel_id=1, source_target_pairs={{0,1},{1,0},{2,3},{3,2},{4,5},{5,4},{6,7},{7,6},{8,9},{9,8},{10,11... | collective-permute-start | bytes 786440 | tf_op jit(solution)/shard_map/ppermute | solution.py:264
  28.8 12.7 %collective-permute-start = (bf16[1024,128]{1,0:T(8,128)(2,1)}, bf16[1024,128]{1,0:T(8,128)(2,1)S(1)}, u32[]{:S(2)}, u32[]{:S(2)}) collective-permute-start(bf16[1024,128]{1,0:T(8,128)(2,1)} %whiten.1.refs_1_), channel_id=1, source_target_pairs={{1,2},{2,1},{3,4},{4,3},{5,6},{6,5},{7,8},{8,7},{9,10},{10,9},{11,... | collective-permute-start | bytes 786440 | tf_op jit(solution)/shard_map/ppermute | solution.py:265
  35.1 0.7 %copy-start.1 = (bf16[1024,128]{1,0:T(8,128)(2,1)}, bf16[1024,128]{1,0:T(8,128)(2,1)S(1)}, u32[]{:S(2)}) copy-start(bf16[1024,128]{1,0:T(8,128)(2,1)S(1)} %collective-permute-done.1.refs_2_) | copy-start | bytes 786436
  41.5 0.7 %copy-start = (bf16[1024,128]{1,0:T(8,128)(2,1)}, bf16[1024,128]{1,0:T(8,128)(2,1)S(1)}, u32[]{:S(2)}) copy-start(bf16[1024,128]{1,0:T(8,128)(2,1)S(1)} %collective-permute-done.refs_2_) | copy-start | bytes 786436

commit v2 on v1

--- a/solution.py
+++ b/solution.py
@@ -75,6 +75,10 @@
     return (table / math.sqrt(SEGS * BAND)).astype(jnp.bfloat16)
 
 
+def in_vmem(array):
+    return pltpu.with_memory_space_constraint(array, pltpu.VMEM)
+
+
 def dot(left, right, left_dim=1, right_dim=0):
     return lax.dot_general(
         left, right, (((left_dim,), (right_dim,)), ((), ())), preferred_element_type=F32
@@ -103,7 +107,7 @@
     channels, samples = raw.shape
     return pl.pallas_call(
         sort_kernel,
-        out_shape=jax.ShapeDtypeStruct((channels, samples), BF16),
+        out_shape=pltpu.VMEM((channels, samples), BF16),
         in_specs=[pl.BlockSpec(memory_space=pltpu.VMEM)] * 2,
         out_specs=pl.BlockSpec(memory_space=pltpu.VMEM),
         scratch_shapes=[pltpu.VMEM((channels, samples), BF16)],
@@ -161,12 +165,12 @@
     smooth, scale = smooth_tables()
     return pl.pallas_call(
         whiten_kernel,
-        out_shape=jax.ShapeDtypeStruct((ROWS, 2 * BLOCK), BF16),
+        out_shape=pltpu.VMEM((ROWS, 2 * BLOCK), BF16),
         in_specs=[pl.BlockSpec(memory_space=pltpu.VMEM)] * 5,
         out_specs=pl.BlockSpec(memory_space=pltpu.VMEM),
         scratch_shapes=[pltpu.VMEM((ROWS, 2 * BLOCK), F32)],
         name="whiten",
-    )(x, band, dft, smooth, scale)
+    )(x, *(in_vmem(jnp.asarray(table)) for table in (band, dft, smooth, scale)))
 
 
 def fill_cross(left_at, right_at, cross):
@@ -250,7 +254,7 @@
         ],
         input_output_aliases={4: 0} if held else {},
         name=f"correlate_{swap}",
-    )(tiles, own, other, lag_table(), *held)
+    )(tiles, own, other, in_vmem(jnp.asarray(lag_table())), *held)
 
 
 def per_device(raw, channel_order, tile_list, tile_owner):
@@ -258,12 +262,13 @@
     ordered = sort_rows(raw, channel_order[0])
     parts = ordered.reshape(SEGS, BLOCK, SEG_LEN)
     record = lax.all_to_all(parts, "tm", split_axis=0, concat_axis=0, tiled=True)
-    own = whiten(record.reshape(ROWS, SEG_LEN))
+    record = in_vmem(record.reshape(ROWS, SEG_LEN))
+    own = in_vmem(whiten(record))
     pairs = [(i, i ^ 1) for i in range(count)]
     shifted = [(i, i + 1 if i % 2 else i - 1) for i in range(1, count - 1)]
-    near = lax.ppermute(own, ("grp", "tm"), pairs)
-    far = lax.ppermute(own, ("grp", "tm"), shifted)
-    tiles = tile_list.T
+    near = in_vmem(lax.ppermute(own, ("grp", "tm"), pairs))
+    far = in_vmem(lax.ppermute(own, ("grp", "tm"), shifted))
+    tiles = in_vmem(tile_list.T)
     out = correlate(0, tiles, own, near)
     out = correlate(1, tiles, own, far, (out,))
     return out.reshape(TILE_CAP, BLOCK, BLOCK, LAGS)

time: 47.1 us -> 42.2 us (0.90)
  Pallas kernels: 17.9 us -> 13.2 us
  waiting for transfers between devices: 5.53 us -> 7.04 us
  local copies, waits for them, and re-layouts: 1.38 us -> 0.03 us
    pallas_call x2, Pallas kernels: 8.8 us -> 6.16 us  [the longest x1 4.07 us: whiten(): pl.pallas_call(whiten_kernel, out_shape=pltpu.VMEM((ROWS, 2 * BLOCK), BF1...]
    pallas_call x2, Pallas kernels: 9.1 us -> 7.02 us  [correlate(): pl.pallas_call(lambda *refs: tile_kernel(swap, *refs), out_shape=jax.Shap...]
    ppermute x2, waiting for transfers between devices: 5.53 us -> 7.04 us  [the longest x1 4.1 us: per_device(): near = in_vmem(lax.ppermute(own, ('grp', 'tm'), pairs))]
    unnamed x4 -> x12, local copies, waits for them, and re-layouts: 1.38 us -> 0.03 us
  transfers between devices with their start and end apart: 2 -> 2, of which waited for: 2 -> 2; matrix products, arithmetic and copies ran while one was open for 0% -> 0% of each run, Pallas kernels for 10% -> 8%
where the time goes in v2:
time: 42.2 us; the launch traced here: 42 us
  blocking collectives  19.2 us (45%)
  Pallas kernels  13.2 us (31%)
  waiting for transfers between devices  7.04 us (17%)
  starting transfers between devices  2.55 us (6%)
    all_to_all x1, blocking collectives, per_device(): lax.all_to_all(parts, 'tm', split_axis=0, concat_axis=0, tiled=True)  19.2 us
    pallas_call x2, Pallas kernels, correlate(): pl.pallas_call(lambda *refs: tile_kernel(swap, *refs), out_shape=jax.Shap...  7.02 us
    ppermute x1, waiting for transfers between devices, per_device(): near = in_vmem(lax.ppermute(own, ('grp', 'tm'), pairs))  4.1 us
    pallas_call x1, Pallas kernels, whiten(): pl.pallas_call(whiten_kernel, out_shape=pltpu.VMEM((ROWS, 2 * BLOCK), BF1...  4.07 us
    ppermute x1, waiting for transfers between devices, per_device(): far = in_vmem(lax.ppermute(own, ('grp', 'tm'), shifted))  2.94 us
    pallas_call x1, Pallas kernels, sort_rows(): pl.pallas_call(sort_kernel, out_shape=pltpu.VMEM((channels, samples), BF1...  2.09 us
    ppermute x1, starting transfers between devices, per_device(): far = in_vmem(lax.ppermute(own, ('grp', 'tm'), shifted))  1.91 us
  transfers between devices with their start and end apart: 2, of which 2 were waited for; matrix products, arithmetic and copies ran while one was open for 0% of the time, Pallas kernels for 8%

profile of v2, /device:TPU:24, one launch (start us, length us, event | category | flops | bytes accessed | tf_op | source)
XLA Modules:
  0.0 42.0 jit_solution(4245186182320729895)
XLA Ops:
  0.0 0.0 copy-start.2
  0.0 0.0 copy-start.4
  0.0 0.0 copy-start.3
  0.0 0.0 copy-start
  0.0 0.0 copy-start.1
  0.0 0.0 copy-start.5
  0.0 2.1 %sort_rows.1 = bf16[1024,256]{1,0:T(8,128)(2,1)S(1)} custom-call(s32[8,128]{1,0:T(8,128)} %bitcast.9, f32[1024,256]{1,0:T(8,128)} %raw_ref.1), custom_call_target="tpu_custom_call" | custom-call | tf_op jit(solution)/shard_map/sort_rows/pallas_call | solution.py:108
  2.1 19.2 %all_to_all.5 = bf16[16,64,256]{2,1,0:T(8,128)(2,1)S(1)} all-to-all(bf16[16,64,256]{2,1,0:T(8,128)(2,1)S(1)} %bitcast.5), channel_id=1, replica_groups=mesh['grp'=8,'tm'=16] {'tm'}, dimensions={0} | all-to-all | bytes 1048576 | tf_op jit(solution)/shard_map/all_to_all | solution.py:264
  21.3 0.0 copy-done.2
  21.3 0.0 copy-done.4
  21.3 0.0 copy-done.3
  21.3 0.0 copy-done
  21.3 4.1 %whiten.1.refs_1_ = bf16[1024,128]{1,0:T(8,128)(2,1)S(1)} custom-call(bf16[1024,256]{1,0:T(8,128)(2,1)S(1)} %bitcast.6, bf16[512,256]{1,0:T(8,128)(2,1)S(1)} %copy-done, bf16[256,256]{1,0:T(8,128)(2,1)S(1)} %copy-done.3, bf16[128,256]{1,0:T(8,128)(2,1)S(1)} %copy-done.4, f32[2,128,128]{2,1,0:T(8,128)S(1)} %copy-done.2), custom_call_target="tpu_custom_call" | custom-call | tf_op jit(solution)/shard_map/whiten/pallas_call | solution.py:166
  25.4 0.6 %collective-permute-start.1 = (bf16[1024,128]{1,0:T(8,128)(2,1)S(1)}, bf16[1024,128]{1,0:T(8,128)(2,1)S(1)}, u32[]{:S(2)}, u32[]{:S(2)}) collective-permute-start(bf16[1024,128]{1,0:T(8,128)(2,1)S(1)} %whiten.1.refs_1_), channel_id=1, source_target_pairs={{0,1},{1,0},{2,3},{3,2},{4,5},{5,4},{6,7},{7,6},{8,9},{9,8},{10,11... | collective-permute-start | bytes 786440 | tf_op jit(solution)/shard_map/ppermute | solution.py:269
  26.1 1.9 %collective-permute-start = (bf16[1024,128]{1,0:T(8,128)(2,1)S(1)}, bf16[1024,128]{1,0:T(8,128)(2,1)S(1)}, u32[]{:S(2)}, u32[]{:S(2)}) collective-permute-start(bf16[1024,128]{1,0:T(8,128)(2,1)S(1)} %whiten.1.refs_1_), channel_id=1, source_target_pairs={{1,2},{2,1},{3,4},{4,3},{5,6},{6,5},{7,8},{8,7},{9,10},{10,9},{11,... | collective-permute-start | bytes 786440 | tf_op jit(solution)/shard_map/ppermute | solution.py:270
  28.0 4.1 %collective-permute-done.1.refs_2_ = bf16[1024,128]{1,0:T(8,128)(2,1)S(1)} collective-permute-done((bf16[1024,128]{1,0:T(8,128)(2,1)S(1)}, bf16[1024,128]{1,0:T(8,128)(2,1)S(1)}, u32[]{:S(2)}, u32[]{:S(2)}) %collective-permute-start.1) | collective-permute-done | bytes 262176 | tf_op jit(solution)/shard_map/ppermute | solution.py:269
  32.1 0.0 copy-done.1
  32.1 0.0 copy-done.5
  32.1 3.5 %correlate_0.1.refs_4_ = bf16[2,4096,128]{2,1,0:T(8,128)(2,1)} custom-call(s32[2,255]{1,0:T(2,128)S(1)} %bitcast.7, bf16[1024,128]{1,0:T(8,128)(2,1)S(1)} %whiten.1.refs_1_, bf16[1024,128]{1,0:T(8,128)(2,1)S(1)} %collective-permute-done.1.refs_2_, bf16[128,128]{1,0:T(8,128)(2,1)S(1)} %copy-done.1), custom_call_target="tpu_custom_call" | custom-call | tf_op jit(solution)/shard_map/correlate_0/pallas_call | solution.py:245
  35.6 2.9 %collective-permute-done.refs_2_ = bf16[1024,128]{1,0:T(8,128)(2,1)S(1)} collective-permute-done((bf16[1024,128]{1,0:T(8,128)(2,1)S(1)}, bf16[1024,128]{1,0:T(8,128)(2,1)S(1)}, u32[]{:S(2)}, u32[]{:S(2)}) %collective-permute-start) | collective-permute-done | bytes 262176 | tf_op jit(solution)/shard_map/ppermute | solution.py:270
  38.5 3.5 %correlate_1.1 = bf16[2,4096,128]{2,1,0:T(8,128)(2,1)} custom-call(s32[2,255]{1,0:T(2,128)S(1)} %bitcast.8, bf16[1024,128]{1,0:T(8,128)(2,1)S(1)} %whiten.1.refs_1_, bf16[1024,128]{1,0:T(8,128)(2,1)S(1)} %collective-permute-done.refs_2_, bf16[128,128]{1,0:T(8,128)(2,1)S(1)} %copy-done.1, ...), custom_call_target="tpu_custom_call", output_to_operand_aliasing={{}: (4, {})} | custom-call | tf_op jit(solution)/shard_map/correlate_1/pallas_call | solution.py:245
Async XLA Ops:
  0.0 21.3 %copy-start.2 = (f32[2,128,128]{2,1,0:T(8,128)S(1)}, f32[2,128,128]{2,1,0:T(8,128)}, u32[]{:S(2)}) copy-start(f32[2,128,128]{2,1,0:T(8,128)} %constant.13.clone.scale_ref) | copy-start | bytes 393220
  0.0 21.3 %copy-start.4 = (bf16[128,256]{1,0:T(8,128)(2,1)S(1)}, bf16[128,256]{1,0:T(8,128)(2,1)}, u32[]{:S(2)}) copy-start(bf16[128,256]{1,0:T(8,128)(2,1)} %constant.12.clone.smooth_ref) | copy-start | bytes 196612
  0.0 21.3 %copy-start.3 = (bf16[256,256]{1,0:T(8,128)(2,1)S(1)}, bf16[256,256]{1,0:T(8,128)(2,1)}, u32[]{:S(2)}) copy-start(bf16[256,256]{1,0:T(8,128)(2,1)} %constant.11.clone.dft_ref) | copy-start | bytes 393220
  0.0 21.3 %copy-start = (bf16[512,256]{1,0:T(8,128)(2,1)S(1)}, bf16[512,256]{1,0:T(8,128)(2,1)}, u32[]{:S(2)}) copy-start(bf16[512,256]{1,0:T(8,128)(2,1)} %constant.10.clone.band_ref) | copy-start | bytes 786436
  0.0 32.0 %copy-start.1 = (bf16[128,128]{1,0:T(8,128)(2,1)S(1)}, bf16[128,128]{1,0:T(8,128)(2,1)}, u32[]{:S(2)}) copy-start(bf16[128,128]{1,0:T(8,128)(2,1)} %constant.14.clone.refs_3_) | copy-start | bytes 98308
  0.0 32.0 %copy-start.5 = (s32[255,2]{0,1:T(2,128)S(1)}, s32[255,2]{0,1:T(2,128)}, u32[]{:S(2)}) copy-start(s32[255,2]{0,1:T(2,128)} %param.12) | copy-start | bytes 6124
  25.4 6.7 %collective-permute-start.1 = (bf16[1024,128]{1,0:T(8,128)(2,1)S(1)}, bf16[1024,128]{1,0:T(8,128)(2,1)S(1)}, u32[]{:S(2)}, u32[]{:S(2)}) collective-permute-start(bf16[1024,128]{1,0:T(8,128)(2,1)S(1)} %whiten.1.refs_1_), channel_id=1, source_target_pairs={{0,1},{1,0},{2,3},{3,2},{4,5},{5,4},{6,7},{7,6},{8,9},{9,8},{10,11... | collective-permute-start | bytes 786440 | tf_op jit(solution)/shard_map/ppermute | solution.py:269
  26.1 12.5 %collective-permute-start = (bf16[1024,128]{1,0:T(8,128)(2,1)S(1)}, bf16[1024,128]{1,0:T(8,128)(2,1)S(1)}, u32[]{:S(2)}, u32[]{:S(2)}) collective-permute-start(bf16[1024,128]{1,0:T(8,128)(2,1)S(1)} %whiten.1.refs_1_), channel_id=1, source_target_pairs={{1,2},{2,1},{3,4},{4,3},{5,6},{6,5},{7,8},{8,7},{9,10},{10,9},{11,... | collective-permute-start | bytes 786440 | tf_op jit(solution)/shard_map/ppermute | solution.py:270

commit v3 on v2

--- a/solution.py
+++ b/solution.py
@@ -17,6 +17,8 @@
 BLOCK = 64
 SEGS = 16
 HALF = BAND // 2
+PITCH = 72
+STEP = 4
 ROWS = SEGS * BLOCK
 F32 = jnp.float32
 BF16 = jnp.bfloat16
@@ -43,9 +45,9 @@
 def dft_table():
     freq, part = frequency_rows()
     sample = np.arange(SEG_LEN)
-    angle = ((freq[:, None] + BAND_LO) * sample[None, :] % SEG_LEN) * (2.0 * math.pi / SEG_LEN)
-    table = np.where(part[:, None] == 0, np.cos(angle), -np.sin(angle)).astype(np.float32)
-    return np.concatenate(split_bf16(table), axis=0)
+    angle = (sample[:, None] * (freq[None, :] + BAND_LO) % SEG_LEN) * (2.0 * math.pi / SEG_LEN)
+    table = np.where(part[None, :] == 0, np.cos(angle), -np.sin(angle)).astype(np.float32)
+    return np.concatenate(split_bf16(table), axis=1)
 
 
 def smooth_tables():
@@ -54,14 +56,8 @@
     band = np.arange(BAND)
     total = (BAND - np.abs(band[:, None] - band[None, :])).sum(axis=0).astype(np.float32)
     taper = 0.5 - 0.5 * np.cos((freq + 0.5) * (2.0 * math.pi / BAND))
-    shape = (2 * BAND, 2 * BLOCK)
-    scale = np.stack(
-        [
-            np.broadcast_to((1.0 / total[freq])[:, None], shape),
-            np.broadcast_to(taper[:, None], shape),
-        ]
-    ).astype(np.float32)
-    return np.concatenate([weights, weights], axis=1).astype(jnp.bfloat16), scale
+    scale = np.stack([1.0 / total[freq], taper] * 4).astype(np.float32)
+    return weights.astype(jnp.bfloat16), scale
 
 
 def lag_table():
@@ -118,36 +114,26 @@
 def whiten_kernel(x_ref, band_ref, dft_ref, smooth_ref, scale_ref, out_ref, held):
     low = low_lanes((BAND, 2 * BLOCK))
     half_seg = SEG_LEN // 2
+    rows = 2 * BLOCK
     for pair in range(SEGS // 2):
-        start = pair * 2 * BLOCK
-        x = x_ref[start : start + 2 * BLOCK, :].astype(F32)
+        start = pair * rows
+        stop = start + rows
+        x = x_ref[start:stop, :]
         size = jnp.abs(x)
-        blank = jnp.zeros((BLOCK, half_seg), F32)
-        before = (
-            jnp.abs(x_ref[start - BLOCK : start, half_seg:].astype(F32)) if pair > 0 else blank
-        )
-        stop = start + 2 * BLOCK
-        after = (
-            jnp.abs(x_ref[stop : stop + BLOCK, :half_seg].astype(F32))
-            if pair < SEGS // 2 - 1
-            else blank
-        )
-        before = jnp.concatenate([before, size[:BLOCK, half_seg:]], axis=0)
+        blank = jnp.zeros((BLOCK, half_seg), BF16)
+        before = jnp.abs(x_ref[start - BLOCK : start, half_seg:]) if pair > 0 else blank
+        after = jnp.abs(x_ref[stop : stop + BLOCK, :half_seg]) if stop < ROWS else blank
+        before = jnp.concatenate([before, size[: rows - BLOCK, half_seg:]], axis=0)
         after = jnp.concatenate([size[BLOCK:, :half_seg], after], axis=0)
-        around = jnp.concatenate([before, size, after], axis=1).astype(BF16)
+        around = jnp.concatenate([before, size, after], axis=1)
         mean = dot(around, band_ref[...]) * (1.0 / (2 * NORM_HALF + 1))
-        normed = x / (mean + 1e-05)
-        normed_high = normed.astype(BF16)
-        normed_low = (normed - normed_high.astype(F32)).astype(BF16)
-        both = dot(dft_ref[...], normed_high, 1, 1)
-        spectrum = (both[: 2 * BAND] + both[2 * BAND :]) + dot(
-            dft_ref[: 2 * BAND, :], normed_low, 1, 1
-        )
-        power = spectrum * spectrum
-        power_high = power.astype(BF16)
-        power_low = (power - power_high.astype(F32)).astype(BF16)
-        smoothed = dot(smooth_ref[...], jnp.concatenate([power_high, power_low], axis=0))
-        white = spectrum * (scale_ref[1] / jnp.sqrt(smoothed * scale_ref[0] + 1e-06))
+        normed = (x.astype(F32) / (mean + 1e-05)).astype(BF16)
+        both = dot(normed, dft_ref[...])
+        spectrum = both[:, : 2 * BAND] + both[:, 2 * BAND :]
+        power = (spectrum * spectrum).astype(BF16)
+        smoothed = dot(power, smooth_ref[...])
+        white = spectrum * (scale_ref[1:2, :] * lax.rsqrt(smoothed * scale_ref[0:1, :] + 1e-06))
+        white = white.T
         lower, upper = white[:BAND], white[BAND:]
         turned = pltpu.roll(jnp.where(low, upper, lower), BLOCK, 1)
         first = jnp.where(low, lower, turned)
@@ -187,20 +173,30 @@
         right = jnp.concatenate(
             [jnp.where(low, right, 0.0), jnp.where(low, 0.0, right)], axis=0
         ).astype(BF16)
-        cross[place * 2 * BLOCK : (place + 1) * 2 * BLOCK, :] = dot(left, right, 0, 0)
-
-
-def fill_lags(cross, lag_ref, stage):
+        value = dot(left, right, 0, 0)
+        for part in range(2):
+            cross[pl.ds((2 * place + part) * PITCH, BLOCK), :] = value[part * BLOCK : (part + 1) * BLOCK]
+
+
+def fill_lags(cross, lag_ref, stage, out, sem):
     low = low_lanes((2 * HALF, 2 * BLOCK))
+    copies = []
     for pair in range(BLOCK // 2):
-        first = cross[pl.ds(2 * pair, 2 * HALF, stride=BLOCK), :]
-        second = cross[pl.ds(2 * pair + 1, 2 * HALF, stride=BLOCK), :]
+        first = cross[pl.ds(2 * pair, 2 * HALF, stride=PITCH), :]
+        second = cross[pl.ds(2 * pair + 1, 2 * HALF, stride=PITCH), :]
         turned = pltpu.roll(jnp.where(low, second, first), BLOCK, 1)
         both = jnp.concatenate(
             [jnp.where(low, first, turned), jnp.where(low, turned, second)], axis=0
-        ).astype(BF16)
+        ).T.astype(BF16)
         rows = slice(2 * pair * BLOCK, 2 * (pair + 1) * BLOCK)
-        stage[rows, :] = dot(both, lag_ref[...], 0, 0).astype(BF16)
+        stage[rows, :] = dot(both, lag_ref[...]).astype(BF16)
+        if (pair + 1) % STEP == 0:
+            done = pl.ds((pair + 1 - STEP) * 2 * BLOCK, STEP * 2 * BLOCK)
+            copy = pltpu.make_async_copy(stage.at[done, :], out.at[done, :], sem.at[pair // STEP])
+            copy.start()
+            copies.append(copy)
+    for copy in copies:
+        copy.wait()
 
 
 def diagonal_slot(tiles_ref, own, last):
@@ -231,12 +227,9 @@
         return jnp.where(no_other, own_ref[rows, :].astype(F32), other_ref[rows, :].astype(F32))
 
     fill_cross(left_at, right_at, cross)
-    fill_lags(cross, lag_ref, stage)
     slot = diagonal_slot(tiles_ref, own, last)
     slot = jnp.where(is_diagonal, slot, 1 - slot)
-    copy = pltpu.make_async_copy(stage, out_ref.at[slot], sem)
-    copy.start()
-    copy.wait()
+    fill_lags(cross, lag_ref, stage, out_ref.at[slot], sem)
 
 
 def correlate(swap, tiles, own, other, held=()):
@@ -248,9 +241,9 @@
         in_specs=[vmem] * 4 + [anywhere] * len(held),
         out_specs=anywhere,
         scratch_shapes=[
-            pltpu.VMEM((HALF * 2 * BLOCK, 2 * BLOCK), F32),
+            pltpu.VMEM((HALF * 2 * PITCH, 2 * BLOCK), F32),
             pltpu.VMEM((BLOCK * BLOCK, LAGS), BF16),
-            pltpu.SemaphoreType.DMA,
+            pltpu.SemaphoreType.DMA((BLOCK // 2 // STEP,)),
         ],
         input_output_aliases={4: 0} if held else {},
         name=f"correlate_{swap}",

time: 42.2 us -> 39 us (0.924)
  Pallas kernels: 13.2 us -> 8.77 us
  waiting for transfers between devices: 7.04 us -> 8.18 us
    pallas_call x2, Pallas kernels: 7.02 us -> 4.76 us  [correlate(): pl.pallas_call(lambda *refs: tile_kernel(swap, *refs), out_shape=jax.Shap...]
    pallas_call x1, Pallas kernels: 4.07 us -> 1.92 us  [whiten(): pl.pallas_call(whiten_kernel, out_shape=pltpu.VMEM((ROWS, 2 * BLOCK), BF1...]
    ppermute x1, waiting for transfers between devices: 2.94 us -> 4.08 us  [per_device(): far = in_vmem(lax.ppermute(own, ('grp', 'tm'), shifted))]
  transfers between devices with their start and end apart: 2 -> 2, of which waited for: 2 -> 2; matrix products, arithmetic and copies ran while one was open for 0% -> 0% of each run, Pallas kernels for 8% -> 6%
where the time goes in v3:
time: 39 us; the launch traced here: 38.8 us
  blocking collectives  19.2 us (49%)
  Pallas kernels  8.77 us (22%)
  waiting for transfers between devices  8.18 us (21%)
  starting transfers between devices  2.55 us (7%)
    all_to_all x1, blocking collectives, per_device(): lax.all_to_all(parts, 'tm', split_axis=0, concat_axis=0, tiled=True)  19.2 us
    pallas_call x2, Pallas kernels, correlate(): pl.pallas_call(lambda *refs: tile_kernel(swap, *refs), out_shape=jax.Shap...  4.76 us
    ppermute x1, waiting for transfers between devices, per_device(): near = in_vmem(lax.ppermute(own, ('grp', 'tm'), pairs))  4.1 us
    ppermute x1, waiting for transfers between devices, per_device(): far = in_vmem(lax.ppermute(own, ('grp', 'tm'), shifted))  4.08 us
    pallas_call x1, Pallas kernels, sort_rows(): pl.pallas_call(sort_kernel, out_shape=pltpu.VMEM((channels, samples), BF1...  2.1 us
    pallas_call x1, Pallas kernels, whiten(): pl.pallas_call(whiten_kernel, out_shape=pltpu.VMEM((ROWS, 2 * BLOCK), BF1...  1.92 us
    ppermute x1, starting transfers between devices, per_device(): far = in_vmem(lax.ppermute(own, ('grp', 'tm'), shifted))  1.91 us
  transfers between devices with their start and end apart: 2, of which 2 were waited for; matrix products, arithmetic and copies ran while one was open for 0% of the time, Pallas kernels for 6%

profile of v3, /device:TPU:24, one launch (start us, length us, event | category | flops | bytes accessed | tf_op | source)
XLA Modules:
  0.0 38.8 jit_solution(17441580035293399984)
XLA Ops:
  0.0 0.0 copy-start.5
  0.0 0.0 copy-start.3
  0.0 0.0 copy-start.2
  0.0 0.0 copy-start
  0.0 0.0 copy-start.1
  0.0 0.0 copy-start.4
  0.0 2.1 %sort_rows.1 = bf16[1024,256]{1,0:T(8,128)(2,1)S(1)} custom-call(s32[8,128]{1,0:T(8,128)} %bitcast.9, f32[1024,256]{1,0:T(8,128)} %raw_ref.1), custom_call_target="tpu_custom_call" | custom-call | tf_op jit(solution)/shard_map/sort_rows/pallas_call | solution.py:104
  2.1 19.2 %all_to_all.5 = bf16[16,64,256]{2,1,0:T(8,128)(2,1)S(1)} all-to-all(bf16[16,64,256]{2,1,0:T(8,128)(2,1)S(1)} %bitcast.5), channel_id=1, replica_groups=mesh['grp'=8,'tm'=16] {'tm'}, dimensions={0} | all-to-all | bytes 1048576 | tf_op jit(solution)/shard_map/all_to_all | solution.py:257
  21.3 0.0 copy-done.5
  21.3 0.0 copy-done.3
  21.3 0.0 copy-done.2
  21.3 0.0 copy-done
  21.3 1.9 %whiten.1.refs_1_ = bf16[1024,128]{1,0:T(8,128)(2,1)S(1)} custom-call(bf16[1024,256]{1,0:T(8,128)(2,1)S(1)} %bitcast.6, bf16[512,256]{1,0:T(8,128)(2,1)S(1)} %copy-done, bf16[256,256]{1,0:T(8,128)(2,1)S(1)} %copy-done.2, bf16[128,128]{1,0:T(8,128)(2,1)S(1)} %copy-done.3, f32[8,128]{1,0:T(8,128)S(1)} %copy-done.5), custom_call_target="tpu_custom_call" | custom-call | tf_op jit(solution)/shard_map/whiten/pallas_call | solution.py:152
  23.3 0.6 %collective-permute-start.1 = (bf16[1024,128]{1,0:T(8,128)(2,1)S(1)}, bf16[1024,128]{1,0:T(8,128)(2,1)S(1)}, u32[]{:S(2)}, u32[]{:S(2)}) collective-permute-start(bf16[1024,128]{1,0:T(8,128)(2,1)S(1)} %whiten.1.refs_1_), channel_id=1, source_target_pairs={{0,1},{1,0},{2,3},{3,2},{4,5},{5,4},{6,7},{7,6},{8,9},{9,8},{10,11... | collective-permute-start | bytes 786440 | tf_op jit(solution)/shard_map/ppermute | solution.py:262
  23.9 1.9 %collective-permute-start = (bf16[1024,128]{1,0:T(8,128)(2,1)S(1)}, bf16[1024,128]{1,0:T(8,128)(2,1)S(1)}, u32[]{:S(2)}, u32[]{:S(2)}) collective-permute-start(bf16[1024,128]{1,0:T(8,128)(2,1)S(1)} %whiten.1.refs_1_), channel_id=1, source_target_pairs={{1,2},{2,1},{3,4},{4,3},{5,6},{6,5},{7,8},{8,7},{9,10},{10,9},{11,... | collective-permute-start | bytes 786440 | tf_op jit(solution)/shard_map/ppermute | solution.py:263
  25.8 4.1 %collective-permute-done.1.refs_2_ = bf16[1024,128]{1,0:T(8,128)(2,1)S(1)} collective-permute-done((bf16[1024,128]{1,0:T(8,128)(2,1)S(1)}, bf16[1024,128]{1,0:T(8,128)(2,1)S(1)}, u32[]{:S(2)}, u32[]{:S(2)}) %collective-permute-start.1) | collective-permute-done | bytes 262176 | tf_op jit(solution)/shard_map/ppermute | solution.py:262
  29.9 0.0 copy-done.1
  29.9 0.0 copy-done.4
  29.9 2.4 %correlate_0.1.refs_4_ = bf16[2,4096,128]{2,1,0:T(8,128)(2,1)} custom-call(s32[2,255]{1,0:T(2,128)S(1)} %bitcast.7, bf16[1024,128]{1,0:T(8,128)(2,1)S(1)} %whiten.1.refs_1_, bf16[1024,128]{1,0:T(8,128)(2,1)S(1)} %collective-permute-done.1.refs_2_, bf16[128,128]{1,0:T(8,128)(2,1)S(1)} %copy-done.1), custom_call_target="tpu_custom_call" | custom-call | tf_op jit(solution)/shard_map/correlate_0/pallas_call | solution.py:238
  32.3 4.1 %collective-permute-done.refs_2_ = bf16[1024,128]{1,0:T(8,128)(2,1)S(1)} collective-permute-done((bf16[1024,128]{1,0:T(8,128)(2,1)S(1)}, bf16[1024,128]{1,0:T(8,128)(2,1)S(1)}, u32[]{:S(2)}, u32[]{:S(2)}) %collective-permute-start) | collective-permute-done | bytes 262176 | tf_op jit(solution)/shard_map/ppermute | solution.py:263
  36.4 2.4 %correlate_1.1 = bf16[2,4096,128]{2,1,0:T(8,128)(2,1)} custom-call(s32[2,255]{1,0:T(2,128)S(1)} %bitcast.8, bf16[1024,128]{1,0:T(8,128)(2,1)S(1)} %whiten.1.refs_1_, bf16[1024,128]{1,0:T(8,128)(2,1)S(1)} %collective-permute-done.refs_2_, bf16[128,128]{1,0:T(8,128)(2,1)S(1)} %copy-done.1, ...), custom_call_target="tpu_custom_call", output_to_operand_aliasing={{}: (4, {})} | custom-call | tf_op jit(solution)/shard_map/correlate_1/pallas_call | solution.py:238
Async XLA Ops:
  0.0 21.3 %copy-start.5 = (f32[8,128]{1,0:T(8,128)S(1)}, f32[8,128]{1,0:T(8,128)}, u32[]{:S(2)}) copy-start(f32[8,128]{1,0:T(8,128)} %constant.13.clone.scale_ref) | copy-start | bytes 12292
  0.0 21.3 %copy-start.3 = (bf16[128,128]{1,0:T(8,128)(2,1)S(1)}, bf16[128,128]{1,0:T(8,128)(2,1)}, u32[]{:S(2)}) copy-start(bf16[128,128]{1,0:T(8,128)(2,1)} %constant.12.clone.smooth_ref) | copy-start | bytes 98308
  0.0 21.3 %copy-start.2 = (bf16[256,256]{1,0:T(8,128)(2,1)S(1)}, bf16[256,256]{1,0:T(8,128)(2,1)}, u32[]{:S(2)}) copy-start(bf16[256,256]{1,0:T(8,128)(2,1)} %constant.11.clone.dft_ref) | copy-start | bytes 393220
  0.0 21.3 %copy-start = (bf16[512,256]{1,0:T(8,128)(2,1)S(1)}, bf16[512,256]{1,0:T(8,128)(2,1)}, u32[]{:S(2)}) copy-start(bf16[512,256]{1,0:T(8,128)(2,1)} %constant.10.clone.band_ref) | copy-start | bytes 786436
  0.0 29.9 %copy-start.1 = (bf16[128,128]{1,0:T(8,128)(2,1)S(1)}, bf16[128,128]{1,0:T(8,128)(2,1)}, u32[]{:S(2)}) copy-start(bf16[128,128]{1,0:T(8,128)(2,1)} %constant.14.clone.refs_3_) | copy-start | bytes 98308
  0.0 29.9 %copy-start.4 = (s32[255,2]{0,1:T(2,128)S(1)}, s32[255,2]{0,1:T(2,128)}, u32[]{:S(2)}) copy-start(s32[255,2]{0,1:T(2,128)} %param.12) | copy-start | bytes 6124
  23.3 6.7 %collective-permute-start.1 = (bf16[1024,128]{1,0:T(8,128)(2,1)S(1)}, bf16[1024,128]{1,0:T(8,128)(2,1)S(1)}, u32[]{:S(2)}, u32[]{:S(2)}) collective-permute-start(bf16[1024,128]{1,0:T(8,128)(2,1)S(1)} %whiten.1.refs_1_), channel_id=1, source_target_pairs={{0,1},{1,0},{2,3},{3,2},{4,5},{5,4},{6,7},{7,6},{8,9},{9,8},{10,11... | collective-permute-start | bytes 786440 | tf_op jit(solution)/shard_map/ppermute | solution.py:262
  23.9 12.5 %collective-permute-start = (bf16[1024,128]{1,0:T(8,128)(2,1)S(1)}, bf16[1024,128]{1,0:T(8,128)(2,1)S(1)}, u32[]{:S(2)}, u32[]{:S(2)}) collective-permute-start(bf16[1024,128]{1,0:T(8,128)(2,1)S(1)} %whiten.1.refs_1_), channel_id=1, source_target_pairs={{1,2},{2,1},{3,4},{4,3},{5,6},{6,5},{7,8},{8,7},{9,10},{10,9},{11,... | collective-permute-start | bytes 786440 | tf_op jit(solution)/shard_map/ppermute | solution.py:263

commit v4 on v3

--- a/solution.py
+++ b/solution.py
@@ -19,6 +19,8 @@
 HALF = BAND // 2
 PITCH = 72
 STEP = 4
+CHUNK = 1024
+PITCH2 = 40
 ROWS = SEGS * BLOCK
 F32 = jnp.float32
 BF16 = jnp.bfloat16
@@ -114,14 +116,13 @@
 def whiten_kernel(x_ref, band_ref, dft_ref, smooth_ref, scale_ref, out_ref, held):
     low = low_lanes((BAND, 2 * BLOCK))
     half_seg = SEG_LEN // 2
-    rows = 2 * BLOCK
-    for pair in range(SEGS // 2):
-        start = pair * rows
+    rows = CHUNK
+    blank = jnp.zeros((BLOCK, half_seg), BF16)
+    for start in range(0, ROWS, rows):
         stop = start + rows
         x = x_ref[start:stop, :]
         size = jnp.abs(x)
-        blank = jnp.zeros((BLOCK, half_seg), BF16)
-        before = jnp.abs(x_ref[start - BLOCK : start, half_seg:]) if pair > 0 else blank
+        before = jnp.abs(x_ref[start - BLOCK : start, half_seg:]) if start > 0 else blank
         after = jnp.abs(x_ref[stop : stop + BLOCK, :half_seg]) if stop < ROWS else blank
         before = jnp.concatenate([before, size[: rows - BLOCK, half_seg:]], axis=0)
         after = jnp.concatenate([size[BLOCK:, :half_seg], after], axis=0)
@@ -132,18 +133,23 @@
         spectrum = both[:, : 2 * BAND] + both[:, 2 * BAND :]
         power = (spectrum * spectrum).astype(BF16)
         smoothed = dot(power, smooth_ref[...])
-        white = spectrum * (scale_ref[1:2, :] * lax.rsqrt(smoothed * scale_ref[0:1, :] + 1e-06))
-        white = white.T
-        lower, upper = white[:BAND], white[BAND:]
-        turned = pltpu.roll(jnp.where(low, upper, lower), BLOCK, 1)
-        first = jnp.where(low, lower, turned)
-        second = jnp.where(low, turned, upper)
-        for segment, value in ((2 * pair, first), (2 * pair + 1, second)):
-            for part in range(2):
-                held[pl.ds(part * SEGS + segment, HALF, stride=2 * SEGS), :] = value[
-                    part * HALF : (part + 1) * HALF
-                ]
-    out_ref[...] = held[...].astype(BF16)
+        whites = spectrum * (scale_ref[1:2, :] * lax.rsqrt(smoothed * scale_ref[0:1, :] + 1e-06))
+        for inner in range(0, rows, 2 * BLOCK):
+            segment = (start + inner) // BLOCK
+            white = whites[inner : inner + 2 * BLOCK].T
+            lower, upper = white[:BAND], white[BAND:]
+            turned = pltpu.roll(jnp.where(low, upper, lower), BLOCK, 1)
+            first = jnp.where(low, lower, turned)
+            second = jnp.where(low, turned, upper)
+            for number, value in ((segment, first), (segment + 1, second)):
+                for part in range(2):
+                    held[pl.ds(part * SEGS + number, HALF, stride=PITCH2), :] = value[
+                        part * HALF : (part + 1) * HALF
+                    ]
+    for place in range(HALF):
+        out_ref[place * 2 * SEGS : (place + 1) * 2 * SEGS, :] = held[
+            place * PITCH2 : place * PITCH2 + 2 * SEGS, :
+        ].astype(BF16)
 
 
 def whiten(x):
@@ -154,7 +160,7 @@
         out_shape=pltpu.VMEM((ROWS, 2 * BLOCK), BF16),
         in_specs=[pl.BlockSpec(memory_space=pltpu.VMEM)] * 5,
         out_specs=pl.BlockSpec(memory_space=pltpu.VMEM),
-        scratch_shapes=[pltpu.VMEM((ROWS, 2 * BLOCK), F32)],
+        scratch_shapes=[pltpu.VMEM((HALF * PITCH2, 2 * BLOCK), F32)],
         name="whiten",
     )(x, *(in_vmem(jnp.asarray(table)) for table in (band, dft, smooth, scale)))
 

time: 39 us -> 38.2 us (0.979)
  Pallas kernels: 8.77 us -> 8.03 us
    pallas_call x1, Pallas kernels: 1.92 us -> 1.18 us  [whiten(): pl.pallas_call(whiten_kernel, out_shape=pltpu.VMEM((ROWS, 2 * BLOCK), BF1...]
where the time goes in v4:
time: 38.2 us; the launch traced here: 38 us
  blocking collectives  19.2 us (50%)
  waiting for transfers between devices  8.18 us (21%)
  Pallas kernels  8.03 us (21%)
  starting transfers between devices  2.55 us (7%)
    all_to_all x1, blocking collectives, per_device(): lax.all_to_all(parts, 'tm', split_axis=0, concat_axis=0, tiled=True)  19.2 us
    pallas_call x2, Pallas kernels, correlate(): pl.pallas_call(lambda *refs: tile_kernel(swap, *refs), out_shape=jax.Shap...  4.76 us
    ppermute x1, waiting for transfers between devices, per_device(): near = in_vmem(lax.ppermute(own, ('grp', 'tm'), pairs))  4.1 us
    ppermute x1, waiting for transfers between devices, per_device(): far = in_vmem(lax.ppermute(own, ('grp', 'tm'), shifted))  4.09 us
    pallas_call x1, Pallas kernels, sort_rows(): pl.pallas_call(sort_kernel, out_shape=pltpu.VMEM((channels, samples), BF1...  2.1 us
    ppermute x1, starting transfers between devices, per_device(): far = in_vmem(lax.ppermute(own, ('grp', 'tm'), shifted))  1.91 us
    pallas_call x1, Pallas kernels, whiten(): pl.pallas_call(whiten_kernel, out_shape=pltpu.VMEM((ROWS, 2 * BLOCK), BF1...  1.18 us
  transfers between devices with their start and end apart: 2, of which 2 were waited for; matrix products, arithmetic and copies ran while one was open for 0% of the time, Pallas kernels for 6%

profile of v4, /device:TPU:24, one launch (start us, length us, event | category | flops | bytes accessed | tf_op | source)
XLA Modules:
  0.0 38.0 jit_solution(7230461763807149005)
XLA Ops:
  0.0 0.0 copy-start.5
  0.0 0.0 copy-start.3
  0.0 0.0 copy-start.2
  0.0 0.0 copy-start
  0.0 0.0 copy-start.1
  0.0 0.0 copy-start.4
  0.0 2.1 %sort_rows.1 = bf16[1024,256]{1,0:T(8,128)(2,1)S(1)} custom-call(s32[8,128]{1,0:T(8,128)} %bitcast.9, f32[1024,256]{1,0:T(8,128)} %raw_ref.1), custom_call_target="tpu_custom_call" | custom-call | tf_op jit(solution)/shard_map/sort_rows/pallas_call | solution.py:106
  2.1 19.2 %all_to_all.5 = bf16[16,64,256]{2,1,0:T(8,128)(2,1)S(1)} all-to-all(bf16[16,64,256]{2,1,0:T(8,128)(2,1)S(1)} %bitcast.5), channel_id=1, replica_groups=mesh['grp'=8,'tm'=16] {'tm'}, dimensions={0} | all-to-all | bytes 1048576 | tf_op jit(solution)/shard_map/all_to_all | solution.py:263
  21.3 0.0 copy-done.5
  21.3 0.0 copy-done.3
  21.3 0.0 copy-done.2
  21.3 0.0 copy-done
  21.3 1.2 %whiten.1.refs_1_ = bf16[1024,128]{1,0:T(8,128)(2,1)S(1)} custom-call(bf16[1024,256]{1,0:T(8,128)(2,1)S(1)} %bitcast.6, bf16[512,256]{1,0:T(8,128)(2,1)S(1)} %copy-done, bf16[256,256]{1,0:T(8,128)(2,1)S(1)} %copy-done.2, bf16[128,128]{1,0:T(8,128)(2,1)S(1)} %copy-done.3, f32[8,128]{1,0:T(8,128)S(1)} %copy-done.5), custom_call_target="tpu_custom_call" | custom-call | tf_op jit(solution)/shard_map/whiten/pallas_call | solution.py:158
  22.5 0.6 %collective-permute-start.1 = (bf16[1024,128]{1,0:T(8,128)(2,1)S(1)}, bf16[1024,128]{1,0:T(8,128)(2,1)S(1)}, u32[]{:S(2)}, u32[]{:S(2)}) collective-permute-start(bf16[1024,128]{1,0:T(8,128)(2,1)S(1)} %whiten.1.refs_1_), channel_id=1, source_target_pairs={{0,1},{1,0},{2,3},{3,2},{4,5},{5,4},{6,7},{7,6},{8,9},{9,8},{10,11... | collective-permute-start | bytes 786440 | tf_op jit(solution)/shard_map/ppermute | solution.py:268
  23.2 1.9 %collective-permute-start = (bf16[1024,128]{1,0:T(8,128)(2,1)S(1)}, bf16[1024,128]{1,0:T(8,128)(2,1)S(1)}, u32[]{:S(2)}, u32[]{:S(2)}) collective-permute-start(bf16[1024,128]{1,0:T(8,128)(2,1)S(1)} %whiten.1.refs_1_), channel_id=1, source_target_pairs={{1,2},{2,1},{3,4},{4,3},{5,6},{6,5},{7,8},{8,7},{9,10},{10,9},{11,... | collective-permute-start | bytes 786440 | tf_op jit(solution)/shard_map/ppermute | solution.py:269
  25.1 4.1 %collective-permute-done.1.refs_2_ = bf16[1024,128]{1,0:T(8,128)(2,1)S(1)} collective-permute-done((bf16[1024,128]{1,0:T(8,128)(2,1)S(1)}, bf16[1024,128]{1,0:T(8,128)(2,1)S(1)}, u32[]{:S(2)}, u32[]{:S(2)}) %collective-permute-start.1) | collective-permute-done | bytes 262176 | tf_op jit(solution)/shard_map/ppermute | solution.py:268
  29.2 0.0 copy-done.1
  29.2 0.0 copy-done.4
  29.2 2.4 %correlate_0.1.refs_4_ = bf16[2,4096,128]{2,1,0:T(8,128)(2,1)} custom-call(s32[2,255]{1,0:T(2,128)S(1)} %bitcast.7, bf16[1024,128]{1,0:T(8,128)(2,1)S(1)} %whiten.1.refs_1_, bf16[1024,128]{1,0:T(8,128)(2,1)S(1)} %collective-permute-done.1.refs_2_, bf16[128,128]{1,0:T(8,128)(2,1)S(1)} %copy-done.1), custom_call_target="tpu_custom_call" | custom-call | tf_op jit(solution)/shard_map/correlate_0/pallas_call | solution.py:244
  31.6 4.1 %collective-permute-done.refs_2_ = bf16[1024,128]{1,0:T(8,128)(2,1)S(1)} collective-permute-done((bf16[1024,128]{1,0:T(8,128)(2,1)S(1)}, bf16[1024,128]{1,0:T(8,128)(2,1)S(1)}, u32[]{:S(2)}, u32[]{:S(2)}) %collective-permute-start) | collective-permute-done | bytes 262176 | tf_op jit(solution)/shard_map/ppermute | solution.py:269
  35.7 2.4 %correlate_1.1 = bf16[2,4096,128]{2,1,0:T(8,128)(2,1)} custom-call(s32[2,255]{1,0:T(2,128)S(1)} %bitcast.8, bf16[1024,128]{1,0:T(8,128)(2,1)S(1)} %whiten.1.refs_1_, bf16[1024,128]{1,0:T(8,128)(2,1)S(1)} %collective-permute-done.refs_2_, bf16[128,128]{1,0:T(8,128)(2,1)S(1)} %copy-done.1, ...), custom_call_target="tpu_custom_call", output_to_operand_aliasing={{}: (4, {})} | custom-call | tf_op jit(solution)/shard_map/correlate_1/pallas_call | solution.py:244
Async XLA Ops:
  0.0 21.3 %copy-start.5 = (f32[8,128]{1,0:T(8,128)S(1)}, f32[8,128]{1,0:T(8,128)}, u32[]{:S(2)}) copy-start(f32[8,128]{1,0:T(8,128)} %constant.13.clone.scale_ref) | copy-start | bytes 12292
  0.0 21.3 %copy-start.3 = (bf16[128,128]{1,0:T(8,128)(2,1)S(1)}, bf16[128,128]{1,0:T(8,128)(2,1)}, u32[]{:S(2)}) copy-start(bf16[128,128]{1,0:T(8,128)(2,1)} %constant.12.clone.smooth_ref) | copy-start | bytes 98308
  0.0 21.3 %copy-start.2 = (bf16[256,256]{1,0:T(8,128)(2,1)S(1)}, bf16[256,256]{1,0:T(8,128)(2,1)}, u32[]{:S(2)}) copy-start(bf16[256,256]{1,0:T(8,128)(2,1)} %constant.11.clone.dft_ref) | copy-start | bytes 393220
  0.0 21.3 %copy-start = (bf16[512,256]{1,0:T(8,128)(2,1)S(1)}, bf16[512,256]{1,0:T(8,128)(2,1)}, u32[]{:S(2)}) copy-start(bf16[512,256]{1,0:T(8,128)(2,1)} %constant.10.clone.band_ref) | copy-start | bytes 786436
  0.0 29.2 %copy-start.1 = (bf16[128,128]{1,0:T(8,128)(2,1)S(1)}, bf16[128,128]{1,0:T(8,128)(2,1)}, u32[]{:S(2)}) copy-start(bf16[128,128]{1,0:T(8,128)(2,1)} %constant.14.clone.refs_3_) | copy-start | bytes 98308
  0.0 29.2 %copy-start.4 = (s32[255,2]{0,1:T(2,128)S(1)}, s32[255,2]{0,1:T(2,128)}, u32[]{:S(2)}) copy-start(s32[255,2]{0,1:T(2,128)} %param.12) | copy-start | bytes 6124
  22.5 6.7 %collective-permute-start.1 = (bf16[1024,128]{1,0:T(8,128)(2,1)S(1)}, bf16[1024,128]{1,0:T(8,128)(2,1)S(1)}, u32[]{:S(2)}, u32[]{:S(2)}) collective-permute-start(bf16[1024,128]{1,0:T(8,128)(2,1)S(1)} %whiten.1.refs_1_), channel_id=1, source_target_pairs={{0,1},{1,0},{2,3},{3,2},{4,5},{5,4},{6,7},{7,6},{8,9},{9,8},{10,11... | collective-permute-start | bytes 786440 | tf_op jit(solution)/shard_map/ppermute | solution.py:268
  23.2 12.5 %collective-permute-start = (bf16[1024,128]{1,0:T(8,128)(2,1)S(1)}, bf16[1024,128]{1,0:T(8,128)(2,1)S(1)}, u32[]{:S(2)}, u32[]{:S(2)}) collective-permute-start(bf16[1024,128]{1,0:T(8,128)(2,1)S(1)} %whiten.1.refs_1_), channel_id=1, source_target_pairs={{1,2},{2,1},{3,4},{4,3},{5,6},{6,5},{7,8},{8,7},{9,10},{10,9},{11,... | collective-permute-start | bytes 786440 | tf_op jit(solution)/shard_map/ppermute | solution.py:269

commit v5 on v4

--- a/solution.py
+++ b/solution.py
@@ -17,10 +17,10 @@
 BLOCK = 64
 SEGS = 16
 HALF = BAND // 2
-PITCH = 72
+PITCH = 65
 STEP = 4
 CHUNK = 1024
-PITCH2 = 40
+PITCH2 = 33
 ROWS = SEGS * BLOCK
 F32 = jnp.float32
 BF16 = jnp.bfloat16
@@ -87,30 +87,39 @@
     return lax.broadcasted_iota(jnp.int32, shape, 1) < BLOCK
 
 
-def sort_kernel(order_ref, raw_ref, out_ref, raw_low):
-    channels = raw_ref.shape[0]
-    raw_low[...] = raw_ref[...].astype(BF16)
+def pick_kernel(order_ref, out_ref):
     lanes = lax.broadcasted_iota(jnp.int32, (128, 128), 1)
-    for chunk in range(channels // 128):
+    for chunk in range(out_ref.shape[0] // 128):
         wanted = jnp.broadcast_to(order_ref[chunk : chunk + 1, :], (128, 128)).T
-        pieces = [
-            jnp.where(wanted == lanes + 128 * piece, 1.0, 0.0).astype(BF16)
-            for piece in range(channels // 128)
-        ]
-        picked = dot(jnp.concatenate(pieces, axis=1), raw_low[...])
-        out_ref[pl.ds(chunk * 128, 128), :] = picked.astype(BF16)
+        for piece in range(out_ref.shape[1] // 128):
+            out_ref[chunk * 128 : (chunk + 1) * 128, piece * 128 : (piece + 1) * 128] = jnp.where(
+                wanted == lanes + 128 * piece, 1.0, 0.0
+            ).astype(BF16)
+
+
+def sort_kernel(picks_ref, raw_ref, out_ref):
+    out_ref[...] = dot(picks_ref[...], raw_ref[...].astype(BF16)).astype(BF16)
 
 
 def sort_rows(raw, order):
     channels, samples = raw.shape
+    vmem = pl.BlockSpec(memory_space=pltpu.VMEM)
+    picks = pl.pallas_call(
+        pick_kernel,
+        out_shape=pltpu.VMEM((channels, channels), BF16),
+        in_specs=[vmem],
+        out_specs=vmem,
+        compiler_params=pltpu.CompilerParams(vmem_limit_bytes=16 << 20),
+        name="pick_rows",
+    )(in_vmem(order.reshape(channels // 128, 128)))
     return pl.pallas_call(
         sort_kernel,
         out_shape=pltpu.VMEM((channels, samples), BF16),
-        in_specs=[pl.BlockSpec(memory_space=pltpu.VMEM)] * 2,
-        out_specs=pl.BlockSpec(memory_space=pltpu.VMEM),
-        scratch_shapes=[pltpu.VMEM((channels, samples), BF16)],
+        in_specs=[vmem] * 2,
+        out_specs=vmem,
+        compiler_params=pltpu.CompilerParams(vmem_limit_bytes=16 << 20),
         name="sort_rows",
-    )(order.reshape(channels // 128, 128), raw)
+    )(in_vmem(picks), in_vmem(raw))
 
 
 def whiten_kernel(x_ref, band_ref, dft_ref, smooth_ref, scale_ref, out_ref, held):

time: 38.2 us -> 38 us (level)
  Pallas kernels: 8.03 us -> 6.78 us
  local copies, waits for them, and re-layouts: 0.03 us -> 0.82 us
    pallas_call x1, Pallas kernels: 2.1 us -> 0.72 us  [sort_rows(): pl.pallas_call(sort_kernel, out_shape=pltpu.VMEM((channels, samples), BF1...]
    unnamed x12 -> x16, local copies, waits for them, and re-layouts: 0.03 us -> 0.82 us
    pallas_call x0 -> x1, Pallas kernels: none -> 0.47 us  [sort_rows(): pl.pallas_call(pick_kernel, out_shape=pltpu.VMEM((channels, channels), BF...]
where the time goes in v5:
time: 38 us; the launch traced here: 37.8 us
  blocking collectives  19.2 us (51%)
  waiting for transfers between devices  8.36 us (22%)
  Pallas kernels  6.78 us (18%)
  starting transfers between devices  2.55 us (7%)
  local copies, waits for them, and re-layouts  0.82 us (2%)
    all_to_all x1, blocking collectives, per_device(): lax.all_to_all(parts, 'tm', split_axis=0, concat_axis=0, tiled=True)  19.2 us
    pallas_call x2, Pallas kernels, correlate(): pl.pallas_call(lambda *refs: tile_kernel(swap, *refs), out_shape=jax.Shap...  4.41 us
    ppermute x1, waiting for transfers between devices, per_device(): far = in_vmem(lax.ppermute(own, ('grp', 'tm'), shifted))  4.26 us
    ppermute x1, waiting for transfers between devices, per_device(): near = in_vmem(lax.ppermute(own, ('grp', 'tm'), pairs))  4.1 us
    ppermute x1, starting transfers between devices, per_device(): far = in_vmem(lax.ppermute(own, ('grp', 'tm'), shifted))  1.91 us
    pallas_call x1, Pallas kernels, whiten(): pl.pallas_call(whiten_kernel, out_shape=pltpu.VMEM((ROWS, 2 * BLOCK), BF1...  1.18 us
    unnamed x16, local copies, waits for them, and re-layouts  0.82 us
  transfers between devices with their start and end apart: 2, of which 2 were waited for; matrix products, arithmetic and copies ran while one was open for 0% of the time, Pallas kernels for 6%

profile of v5, /device:TPU:24, one launch (start us, length us, event | category | flops | bytes accessed | tf_op | source)
XLA Modules:
  0.0 37.8 jit_solution(1911915308896681387)
XLA Ops:
  0.0 0.0 copy-start
  0.0 0.0 copy-start.6
  0.0 0.8 %copy-done.6 = s32[1,1024]{1,0:T(1,128)S(1)} copy-done((s32[1,1024]{1,0:T(1,128)S(1)}, s32[1,1024]{1,0:T(1,128)}, u32[]{:S(2)}) %copy-start.6) | copy-done | bytes 4120
  0.8 0.5 %pick_rows.1.picks_ref = bf16[1024,1024]{1,0:T(8,128)(2,1)S(1)} custom-call(s32[8,128]{1,0:T(8,128)S(1)} %bitcast.9), custom_call_target="tpu_custom_call" | custom-call | tf_op jit(solution)/shard_map/pick_rows/pallas_call | solution.py:107
  1.3 0.0 copy-done
  1.3 0.0 copy-start.1
  1.3 0.0 copy-start.3
  1.3 0.0 copy-start.4
  1.3 0.0 copy-start.7
  1.3 0.0 copy-start.2
  1.3 0.0 copy-start.5
  1.3 0.7 %sort_rows.1 = bf16[1024,256]{1,0:T(8,128)(2,1)S(1)} custom-call(bf16[1024,1024]{1,0:T(8,128)(2,1)S(1)} %pick_rows.1.picks_ref, f32[1024,256]{1,0:T(8,128)S(1)} %copy-done), custom_call_target="tpu_custom_call" | custom-call | tf_op jit(solution)/shard_map/sort_rows/pallas_call | solution.py:115
  2.1 19.2 %all_to_all.5 = bf16[16,64,256]{2,1,0:T(8,128)(2,1)S(1)} all-to-all(bf16[16,64,256]{2,1,0:T(8,128)(2,1)S(1)} %bitcast.5), channel_id=1, replica_groups=mesh['grp'=8,'tm'=16] {'tm'}, dimensions={0} | all-to-all | bytes 1048576 | tf_op jit(solution)/shard_map/all_to_all | solution.py:272
  21.2 0.0 copy-done.1
  21.2 0.0 copy-done.3
  21.2 0.0 copy-done.4
  21.2 0.0 copy-done.7
  21.3 1.2 %whiten.1.refs_1_ = bf16[1024,128]{1,0:T(8,128)(2,1)S(1)} custom-call(bf16[1024,256]{1,0:T(8,128)(2,1)S(1)} %bitcast.6, bf16[512,256]{1,0:T(8,128)(2,1)S(1)} %copy-done.1, bf16[256,256]{1,0:T(8,128)(2,1)S(1)} %copy-done.3, bf16[128,128]{1,0:T(8,128)(2,1)S(1)} %copy-done.4, f32[8,128]{1,0:T(8,128)S(1)} %copy-done.7), custom_call_target="tpu_custom_call" | custom-call | tf_op jit(solution)/shard_map/whiten/pallas_call | solution.py:167
  22.4 0.6 %collective-permute-start.1 = (bf16[1024,128]{1,0:T(8,128)(2,1)S(1)}, bf16[1024,128]{1,0:T(8,128)(2,1)S(1)}, u32[]{:S(2)}, u32[]{:S(2)}) collective-permute-start(bf16[1024,128]{1,0:T(8,128)(2,1)S(1)} %whiten.1.refs_1_), channel_id=1, source_target_pairs={{0,1},{1,0},{2,3},{3,2},{4,5},{5,4},{6,7},{7,6},{8,9},{9,8},{10,11... | collective-permute-start | bytes 786440 | tf_op jit(solution)/shard_map/ppermute | solution.py:277
  23.1 1.9 %collective-permute-start = (bf16[1024,128]{1,0:T(8,128)(2,1)S(1)}, bf16[1024,128]{1,0:T(8,128)(2,1)S(1)}, u32[]{:S(2)}, u32[]{:S(2)}) collective-permute-start(bf16[1024,128]{1,0:T(8,128)(2,1)S(1)} %whiten.1.refs_1_), channel_id=1, source_target_pairs={{1,2},{2,1},{3,4},{4,3},{5,6},{6,5},{7,8},{8,7},{9,10},{10,9},{11,... | collective-permute-start | bytes 786440 | tf_op jit(solution)/shard_map/ppermute | solution.py:278
  25.0 4.1 %collective-permute-done.1.refs_2_ = bf16[1024,128]{1,0:T(8,128)(2,1)S(1)} collective-permute-done((bf16[1024,128]{1,0:T(8,128)(2,1)S(1)}, bf16[1024,128]{1,0:T(8,128)(2,1)S(1)}, u32[]{:S(2)}, u32[]{:S(2)}) %collective-permute-start.1) | collective-permute-done | bytes 262176 | tf_op jit(solution)/shard_map/ppermute | solution.py:277
  29.1 0.0 copy-done.2
  29.1 0.0 copy-done.5
  29.1 2.2 %correlate_0.1.refs_4_ = bf16[2,4096,128]{2,1,0:T(8,128)(2,1)} custom-call(s32[2,255]{1,0:T(2,128)S(1)} %bitcast.7, bf16[1024,128]{1,0:T(8,128)(2,1)S(1)} %whiten.1.refs_1_, bf16[1024,128]{1,0:T(8,128)(2,1)S(1)} %collective-permute-done.1.refs_2_, bf16[128,128]{1,0:T(8,128)(2,1)S(1)} %copy-done.2), custom_call_target="tpu_custom_call" | custom-call | tf_op jit(solution)/shard_map/correlate_0/pallas_call | solution.py:253
  31.3 4.3 %collective-permute-done.refs_2_ = bf16[1024,128]{1,0:T(8,128)(2,1)S(1)} collective-permute-done((bf16[1024,128]{1,0:T(8,128)(2,1)S(1)}, bf16[1024,128]{1,0:T(8,128)(2,1)S(1)}, u32[]{:S(2)}, u32[]{:S(2)}) %collective-permute-start) | collective-permute-done | bytes 262176 | tf_op jit(solution)/shard_map/ppermute | solution.py:278
  35.6 2.2 %correlate_1.1 = bf16[2,4096,128]{2,1,0:T(8,128)(2,1)} custom-call(s32[2,255]{1,0:T(2,128)S(1)} %bitcast.8, bf16[1024,128]{1,0:T(8,128)(2,1)S(1)} %whiten.1.refs_1_, bf16[1024,128]{1,0:T(8,128)(2,1)S(1)} %collective-permute-done.refs_2_, bf16[128,128]{1,0:T(8,128)(2,1)S(1)} %copy-done.2, ...), custom_call_target="tpu_custom_call", output_to_operand_aliasing={{}: (4, {})} | custom-call | tf_op jit(solution)/shard_map/correlate_1/pallas_call | solution.py:253
Async XLA Ops:
  0.0 1.3 %copy-start = (f32[1024,256]{1,0:T(8,128)S(1)}, f32[1024,256]{1,0:T(8,128)}, u32[]{:S(2)}) copy-start(f32[1024,256]{1,0:T(8,128)} %raw_ref.1) | copy-start | bytes 3145732
  0.0 0.8 %copy-start.6 = (s32[1,1024]{1,0:T(1,128)S(1)}, s32[1,1024]{1,0:T(1,128)}, u32[]{:S(2)}) copy-start(s32[1,1024]{1,0:T(1,128)} %param.11) | copy-start | bytes 12292
  1.3 20.0 %copy-start.1 = (bf16[512,256]{1,0:T(8,128)(2,1)S(1)}, bf16[512,256]{1,0:T(8,128)(2,1)}, u32[]{:S(2)}) copy-start(bf16[512,256]{1,0:T(8,128)(2,1)} %constant.10.clone.band_ref) | copy-start | bytes 786436
  1.3 20.0 %copy-start.3 = (bf16[256,256]{1,0:T(8,128)(2,1)S(1)}, bf16[256,256]{1,0:T(8,128)(2,1)}, u32[]{:S(2)}) copy-start(bf16[256,256]{1,0:T(8,128)(2,1)} %constant.11.clone.dft_ref) | copy-start | bytes 393220
  1.3 19.9 %copy-start.4 = (bf16[128,128]{1,0:T(8,128)(2,1)S(1)}, bf16[128,128]{1,0:T(8,128)(2,1)}, u32[]{:S(2)}) copy-start(bf16[128,128]{1,0:T(8,128)(2,1)} %constant.12.clone.smooth_ref) | copy-start | bytes 98308
  1.3 19.9 %copy-start.7 = (f32[8,128]{1,0:T(8,128)S(1)}, f32[8,128]{1,0:T(8,128)}, u32[]{:S(2)}) copy-start(f32[8,128]{1,0:T(8,128)} %constant.13.clone.scale_ref) | copy-start | bytes 12292
  1.3 27.8 %copy-start.2 = (bf16[128,128]{1,0:T(8,128)(2,1)S(1)}, bf16[128,128]{1,0:T(8,128)(2,1)}, u32[]{:S(2)}) copy-start(bf16[128,128]{1,0:T(8,128)(2,1)} %constant.14.clone.refs_3_) | copy-start | bytes 98308
  1.3 27.8 %copy-start.5 = (s32[255,2]{0,1:T(2,128)S(1)}, s32[255,2]{0,1:T(2,128)}, u32[]{:S(2)}) copy-start(s32[255,2]{0,1:T(2,128)} %param.12) | copy-start | bytes 6124
  22.4 6.7 %collective-permute-start.1 = (bf16[1024,128]{1,0:T(8,128)(2,1)S(1)}, bf16[1024,128]{1,0:T(8,128)(2,1)S(1)}, u32[]{:S(2)}, u32[]{:S(2)}) collective-permute-start(bf16[1024,128]{1,0:T(8,128)(2,1)S(1)} %whiten.1.refs_1_), channel_id=1, source_target_pairs={{0,1},{1,0},{2,3},{3,2},{4,5},{5,4},{6,7},{7,6},{8,9},{9,8},{10,11... | collective-permute-start | bytes 786440 | tf_op jit(solution)/shard_map/ppermute | solution.py:277
  23.1 12.5 %collective-permute-start = (bf16[1024,128]{1,0:T(8,128)(2,1)S(1)}, bf16[1024,128]{1,0:T(8,128)(2,1)S(1)}, u32[]{:S(2)}, u32[]{:S(2)}) collective-permute-start(bf16[1024,128]{1,0:T(8,128)(2,1)S(1)} %whiten.1.refs_1_), channel_id=1, source_target_pairs={{1,2},{2,1},{3,4},{4,3},{5,6},{6,5},{7,8},{8,7},{9,10},{10,9},{11,... | collective-permute-start | bytes 786440 | tf_op jit(solution)/shard_map/ppermute | solution.py:278

commit v6 on v5

--- a/solution.py
+++ b/solution.py
@@ -70,7 +70,11 @@
     angle = (freq[:, None] * lag[None, :] % SEG_LEN) * (2.0 * math.pi / SEG_LEN)
     table = np.where(part[:, None] == 0, np.cos(angle), -np.sin(angle))
     table = table.astype(np.float32).astype(jnp.bfloat16).astype(np.float32)
-    return (table / math.sqrt(SEGS * BAND)).astype(jnp.bfloat16)
+    table = table / math.sqrt(SEGS * BAND)
+    both = np.zeros((2, 2, BAND, 2, LAGS), np.float32)
+    for channel in range(2):
+        both[:, channel, :, channel, :] = table.reshape(2, BAND, LAGS)
+    return both.reshape(4 * BAND, 2 * LAGS).astype(jnp.bfloat16)
 
 
 def in_vmem(array):
@@ -194,17 +198,20 @@
 
 
 def fill_lags(cross, lag_ref, stage, out, sem):
-    low = low_lanes((2 * HALF, 2 * BLOCK))
     copies = []
-    for pair in range(BLOCK // 2):
-        first = cross[pl.ds(2 * pair, 2 * HALF, stride=PITCH), :]
-        second = cross[pl.ds(2 * pair + 1, 2 * HALF, stride=PITCH), :]
-        turned = pltpu.roll(jnp.where(low, second, first), BLOCK, 1)
-        both = jnp.concatenate(
-            [jnp.where(low, first, turned), jnp.where(low, turned, second)], axis=0
-        ).T.astype(BF16)
-        rows = slice(2 * pair * BLOCK, 2 * (pair + 1) * BLOCK)
-        stage[rows, :] = dot(both, lag_ref[...]).astype(BF16)
+    for pair in range(1, BLOCK // 2, 2):
+        lefts = []
+        for each in range(pair - 1, pair + 1):
+            first = cross[pl.ds(2 * each, 2 * HALF, stride=PITCH), :]
+            second = cross[pl.ds(2 * each + 1, 2 * HALF, stride=PITCH), :]
+            turned = jnp.concatenate([first, second], axis=0).astype(BF16).T
+            lefts.append(jnp.concatenate([turned[:BLOCK], turned[BLOCK:]], axis=1))
+        values = dot(jnp.concatenate(lefts, axis=0), lag_ref[...]).astype(BF16)
+        for number in range(2):
+            rows = values[number * BLOCK : (number + 1) * BLOCK]
+            start = 2 * (pair - 1 + number) * BLOCK
+            stage[start : start + BLOCK, :] = rows[:, :LAGS]
+            stage[start + BLOCK : start + 2 * BLOCK, :] = rows[:, LAGS:]
         if (pair + 1) % STEP == 0:
             done = pl.ds((pair + 1 - STEP) * 2 * BLOCK, STEP * 2 * BLOCK)
             copy = pltpu.make_async_copy(stage.at[done, :], out.at[done, :], sem.at[pair // STEP])

time: 38 us -> 37.9 us (level)
  no operation moved by 1% of the time
where the time goes in v6:
time: 37.9 us; the launch traced here: 37.7 us
  blocking collectives  19.2 us (51%)
  waiting for transfers between devices  8.45 us (22%)
  Pallas kernels  6.58 us (17%)
  starting transfers between devices  2.55 us (7%)
  local copies, waits for them, and re-layouts  0.82 us (2%)
    all_to_all x1, blocking collectives, per_device(): lax.all_to_all(parts, 'tm', split_axis=0, concat_axis=0, tiled=True)  19.2 us
    ppermute x1, waiting for transfers between devices, per_device(): far = in_vmem(lax.ppermute(own, ('grp', 'tm'), shifted))  4.35 us
    pallas_call x2, Pallas kernels, correlate(): pl.pallas_call(lambda *refs: tile_kernel(swap, *refs), out_shape=jax.Shap...  4.22 us
    ppermute x1, waiting for transfers between devices, per_device(): near = in_vmem(lax.ppermute(own, ('grp', 'tm'), pairs))  4.1 us
    ppermute x1, starting transfers between devices, per_device(): far = in_vmem(lax.ppermute(own, ('grp', 'tm'), shifted))  1.91 us
    pallas_call x1, Pallas kernels, whiten(): pl.pallas_call(whiten_kernel, out_shape=pltpu.VMEM((ROWS, 2 * BLOCK), BF1...  1.18 us
    unnamed x16, local copies, waits for them, and re-layouts  0.82 us
  transfers between devices with their start and end apart: 2, of which 2 were waited for; matrix products, arithmetic and copies ran while one was open for 0% of the time, Pallas kernels for 6%

profile of v6, /device:TPU:24, one launch (start us, length us, event | category | flops | bytes accessed | tf_op | source)
XLA Modules:
  0.0 37.7 jit_solution(639068892740483562)
XLA Ops:
  0.0 0.0 copy-start
  0.0 0.0 copy-start.6
  0.0 0.8 %copy-done.6 = s32[1,1024]{1,0:T(1,128)S(1)} copy-done((s32[1,1024]{1,0:T(1,128)S(1)}, s32[1,1024]{1,0:T(1,128)}, u32[]{:S(2)}) %copy-start.6) | copy-done | bytes 4120
  0.8 0.5 %pick_rows.1.picks_ref = bf16[1024,1024]{1,0:T(8,128)(2,1)S(1)} custom-call(s32[8,128]{1,0:T(8,128)S(1)} %bitcast.9), custom_call_target="tpu_custom_call" | custom-call | tf_op jit(solution)/shard_map/pick_rows/pallas_call | solution.py:111
  1.3 0.0 copy-done
  1.3 0.0 copy-start.2
  1.3 0.0 copy-start.3
  1.3 0.0 copy-start.4
  1.3 0.0 copy-start.7
  1.3 0.0 copy-start.1
  1.3 0.0 copy-start.5
  1.3 0.7 %sort_rows.1 = bf16[1024,256]{1,0:T(8,128)(2,1)S(1)} custom-call(bf16[1024,1024]{1,0:T(8,128)(2,1)S(1)} %pick_rows.1.picks_ref, f32[1024,256]{1,0:T(8,128)S(1)} %copy-done), custom_call_target="tpu_custom_call" | custom-call | tf_op jit(solution)/shard_map/sort_rows/pallas_call | solution.py:119
  2.1 19.2 %all_to_all.5 = bf16[16,64,256]{2,1,0:T(8,128)(2,1)S(1)} all-to-all(bf16[16,64,256]{2,1,0:T(8,128)(2,1)S(1)} %bitcast.5), channel_id=1, replica_groups=mesh['grp'=8,'tm'=16] {'tm'}, dimensions={0} | all-to-all | bytes 1048576 | tf_op jit(solution)/shard_map/all_to_all | solution.py:279
  21.2 0.0 copy-done.2
  21.2 0.0 copy-done.3
  21.2 0.0 copy-done.4
  21.2 0.0 copy-done.7
  21.3 1.2 %whiten.1.refs_1_ = bf16[1024,128]{1,0:T(8,128)(2,1)S(1)} custom-call(bf16[1024,256]{1,0:T(8,128)(2,1)S(1)} %bitcast.6, bf16[512,256]{1,0:T(8,128)(2,1)S(1)} %copy-done.2, bf16[256,256]{1,0:T(8,128)(2,1)S(1)} %copy-done.3, bf16[128,128]{1,0:T(8,128)(2,1)S(1)} %copy-done.4, f32[8,128]{1,0:T(8,128)S(1)} %copy-done.7), custom_call_target="tpu_custom_call" | custom-call | tf_op jit(solution)/shard_map/whiten/pallas_call | solution.py:171
  22.4 0.6 %collective-permute-start.1 = (bf16[1024,128]{1,0:T(8,128)(2,1)S(1)}, bf16[1024,128]{1,0:T(8,128)(2,1)S(1)}, u32[]{:S(2)}, u32[]{:S(2)}) collective-permute-start(bf16[1024,128]{1,0:T(8,128)(2,1)S(1)} %whiten.1.refs_1_), channel_id=1, source_target_pairs={{0,1},{1,0},{2,3},{3,2},{4,5},{5,4},{6,7},{7,6},{8,9},{9,8},{10,11... | collective-permute-start | bytes 786440 | tf_op jit(solution)/shard_map/ppermute | solution.py:284
  23.1 1.9 %collective-permute-start = (bf16[1024,128]{1,0:T(8,128)(2,1)S(1)}, bf16[1024,128]{1,0:T(8,128)(2,1)S(1)}, u32[]{:S(2)}, u32[]{:S(2)}) collective-permute-start(bf16[1024,128]{1,0:T(8,128)(2,1)S(1)} %whiten.1.refs_1_), channel_id=1, source_target_pairs={{1,2},{2,1},{3,4},{4,3},{5,6},{6,5},{7,8},{8,7},{9,10},{10,9},{11,... | collective-permute-start | bytes 786440 | tf_op jit(solution)/shard_map/ppermute | solution.py:285
  25.0 4.1 %collective-permute-done.1.refs_2_ = bf16[1024,128]{1,0:T(8,128)(2,1)S(1)} collective-permute-done((bf16[1024,128]{1,0:T(8,128)(2,1)S(1)}, bf16[1024,128]{1,0:T(8,128)(2,1)S(1)}, u32[]{:S(2)}, u32[]{:S(2)}) %collective-permute-start.1) | collective-permute-done | bytes 262176 | tf_op jit(solution)/shard_map/ppermute | solution.py:284
  29.1 0.0 copy-done.1
  29.1 0.0 copy-done.5
  29.1 2.1 %correlate_0.1.refs_4_ = bf16[2,4096,128]{2,1,0:T(8,128)(2,1)} custom-call(s32[2,255]{1,0:T(2,128)S(1)} %bitcast.7, bf16[1024,128]{1,0:T(8,128)(2,1)S(1)} %whiten.1.refs_1_, bf16[1024,128]{1,0:T(8,128)(2,1)S(1)} %collective-permute-done.1.refs_2_, bf16[256,256]{1,0:T(8,128)(2,1)S(1)} %copy-done.1), custom_call_target="tpu_custom_call" | custom-call | tf_op jit(solution)/shard_map/correlate_0/pallas_call | solution.py:260
  31.2 4.3 %collective-permute-done.refs_2_ = bf16[1024,128]{1,0:T(8,128)(2,1)S(1)} collective-permute-done((bf16[1024,128]{1,0:T(8,128)(2,1)S(1)}, bf16[1024,128]{1,0:T(8,128)(2,1)S(1)}, u32[]{:S(2)}, u32[]{:S(2)}) %collective-permute-start) | collective-permute-done | bytes 262176 | tf_op jit(solution)/shard_map/ppermute | solution.py:285
  35.6 2.1 %correlate_1.1 = bf16[2,4096,128]{2,1,0:T(8,128)(2,1)} custom-call(s32[2,255]{1,0:T(2,128)S(1)} %bitcast.8, bf16[1024,128]{1,0:T(8,128)(2,1)S(1)} %whiten.1.refs_1_, bf16[1024,128]{1,0:T(8,128)(2,1)S(1)} %collective-permute-done.refs_2_, bf16[256,256]{1,0:T(8,128)(2,1)S(1)} %copy-done.1, ...), custom_call_target="tpu_custom_call", output_to_operand_aliasing={{}: (4, {})} | custom-call | tf_op jit(solution)/shard_map/correlate_1/pallas_call | solution.py:260
Async XLA Ops:
  0.0 1.3 %copy-start = (f32[1024,256]{1,0:T(8,128)S(1)}, f32[1024,256]{1,0:T(8,128)}, u32[]{:S(2)}) copy-start(f32[1024,256]{1,0:T(8,128)} %raw_ref.1) | copy-start | bytes 3145732
  0.0 0.8 %copy-start.6 = (s32[1,1024]{1,0:T(1,128)S(1)}, s32[1,1024]{1,0:T(1,128)}, u32[]{:S(2)}) copy-start(s32[1,1024]{1,0:T(1,128)} %param.11) | copy-start | bytes 12292
  1.3 20.0 %copy-start.2 = (bf16[512,256]{1,0:T(8,128)(2,1)S(1)}, bf16[512,256]{1,0:T(8,128)(2,1)}, u32[]{:S(2)}) copy-start(bf16[512,256]{1,0:T(8,128)(2,1)} %constant.10.clone.band_ref) | copy-start | bytes 786436
  1.3 20.0 %copy-start.3 = (bf16[256,256]{1,0:T(8,128)(2,1)S(1)}, bf16[256,256]{1,0:T(8,128)(2,1)}, u32[]{:S(2)}) copy-start(bf16[256,256]{1,0:T(8,128)(2,1)} %constant.11.clone.dft_ref) | copy-start | bytes 393220
  1.3 19.9 %copy-start.4 = (bf16[128,128]{1,0:T(8,128)(2,1)S(1)}, bf16[128,128]{1,0:T(8,128)(2,1)}, u32[]{:S(2)}) copy-start(bf16[128,128]{1,0:T(8,128)(2,1)} %constant.12.clone.smooth_ref) | copy-start | bytes 98308
  1.3 19.9 %copy-start.7 = (f32[8,128]{1,0:T(8,128)S(1)}, f32[8,128]{1,0:T(8,128)}, u32[]{:S(2)}) copy-start(f32[8,128]{1,0:T(8,128)} %constant.13.clone.scale_ref) | copy-start | bytes 12292
  1.3 27.8 %copy-start.1 = (bf16[256,256]{1,0:T(8,128)(2,1)S(1)}, bf16[256,256]{1,0:T(8,128)(2,1)}, u32[]{:S(2)}) copy-start(bf16[256,256]{1,0:T(8,128)(2,1)} %constant.14.clone.refs_3_) | copy-start | bytes 393220
  1.3 27.8 %copy-start.5 = (s32[255,2]{0,1:T(2,128)S(1)}, s32[255,2]{0,1:T(2,128)}, u32[]{:S(2)}) copy-start(s32[255,2]{0,1:T(2,128)} %param.12) | copy-start | bytes 6124
  22.4 6.7 %collective-permute-start.1 = (bf16[1024,128]{1,0:T(8,128)(2,1)S(1)}, bf16[1024,128]{1,0:T(8,128)(2,1)S(1)}, u32[]{:S(2)}, u32[]{:S(2)}) collective-permute-start(bf16[1024,128]{1,0:T(8,128)(2,1)S(1)} %whiten.1.refs_1_), channel_id=1, source_target_pairs={{0,1},{1,0},{2,3},{3,2},{4,5},{5,4},{6,7},{7,6},{8,9},{9,8},{10,11... | collective-permute-start | bytes 786440 | tf_op jit(solution)/shard_map/ppermute | solution.py:284
  23.1 12.5 %collective-permute-start = (bf16[1024,128]{1,0:T(8,128)(2,1)S(1)}, bf16[1024,128]{1,0:T(8,128)(2,1)S(1)}, u32[]{:S(2)}, u32[]{:S(2)}) collective-permute-start(bf16[1024,128]{1,0:T(8,128)(2,1)S(1)} %whiten.1.refs_1_), channel_id=1, source_target_pairs={{1,2},{2,1},{3,4},{4,3},{5,6},{6,5},{7,8},{8,7},{9,10},{10,9},{11,... | collective-permute-start | bytes 786440 | tf_op jit(solution)/shard_map/ppermute | solution.py:285

commit v7 on v6

--- a/solution.py
+++ b/solution.py
@@ -18,7 +18,7 @@
 SEGS = 16
 HALF = BAND // 2
 PITCH = 65
-STEP = 4
+STEP = 8
 CHUNK = 1024
 PITCH2 = 33
 ROWS = SEGS * BLOCK
@@ -173,7 +173,7 @@
         out_shape=pltpu.VMEM((ROWS, 2 * BLOCK), BF16),
         in_specs=[pl.BlockSpec(memory_space=pltpu.VMEM)] * 5,
         out_specs=pl.BlockSpec(memory_space=pltpu.VMEM),
-        scratch_shapes=[pltpu.VMEM((HALF * PITCH2, 2 * BLOCK), F32)],
+        scratch_shapes=[pltpu.VMEM(((HALF + 2) * PITCH2 // 8 * 8, 2 * BLOCK), F32)],
         name="whiten",
     )(x, *(in_vmem(jnp.asarray(table)) for table in (band, dft, smooth, scale)))
 
@@ -263,7 +263,7 @@
         in_specs=[vmem] * 4 + [anywhere] * len(held),
         out_specs=anywhere,
         scratch_shapes=[
-            pltpu.VMEM((HALF * 2 * PITCH, 2 * BLOCK), F32),
+            pltpu.VMEM(((2 * HALF + 2) * PITCH // 8 * 8, 2 * BLOCK), F32),
             pltpu.VMEM((BLOCK * BLOCK, LAGS), BF16),
             pltpu.SemaphoreType.DMA((BLOCK // 2 // STEP,)),
         ],

time: 37.9 us -> 37.8 us (level)
  no operation moved by 1% of the time
where the time goes in v7:
time: 37.8 us; the launch traced here: 37.7 us
  blocking collectives  19.2 us (51%)
  waiting for transfers between devices  8.47 us (22%)
  Pallas kernels  6.53 us (17%)
  starting transfers between devices  2.55 us (7%)
  local copies, waits for them, and re-layouts  0.82 us (2%)
    all_to_all x1, blocking collectives, per_device(): lax.all_to_all(parts, 'tm', split_axis=0, concat_axis=0, tiled=True)  19.2 us
    ppermute x1, waiting for transfers between devices, per_device(): far = in_vmem(lax.ppermute(own, ('grp', 'tm'), shifted))  4.37 us
    pallas_call x2, Pallas kernels, correlate(): pl.pallas_call(lambda *refs: tile_kernel(swap, *refs), out_shape=jax.Shap...  4.16 us
    ppermute x1, waiting for transfers between devices, per_device(): near = in_vmem(lax.ppermute(own, ('grp', 'tm'), pairs))  4.1 us
    ppermute x1, starting transfers between devices, per_device(): far = in_vmem(lax.ppermute(own, ('grp', 'tm'), shifted))  1.91 us
    pallas_call x1, Pallas kernels, whiten(): pl.pallas_call(whiten_kernel, out_shape=pltpu.VMEM((ROWS, 2 * BLOCK), BF1...  1.18 us
    unnamed x16, local copies, waits for them, and re-layouts  0.82 us
  transfers between devices with their start and end apart: 2, of which 2 were waited for; matrix products, arithmetic and copies ran while one was open for 0% of the time, Pallas kernels for 6%

profile of v7, /device:TPU:24, one launch (start us, length us, event | category | flops | bytes accessed | tf_op | source)
XLA Modules:
  0.0 37.7 jit_solution(10315477022433003811)
XLA Ops:
  0.0 0.0 copy-start
  0.0 0.0 copy-start.6
  0.0 0.8 %copy-done.6 = s32[1,1024]{1,0:T(1,128)S(1)} copy-done((s32[1,1024]{1,0:T(1,128)S(1)}, s32[1,1024]{1,0:T(1,128)}, u32[]{:S(2)}) %copy-start.6) | copy-done | bytes 4120
  0.8 0.5 %pick_rows.1.picks_ref = bf16[1024,1024]{1,0:T(8,128)(2,1)S(1)} custom-call(s32[8,128]{1,0:T(8,128)S(1)} %bitcast.9), custom_call_target="tpu_custom_call" | custom-call | tf_op jit(solution)/shard_map/pick_rows/pallas_call | solution.py:111
  1.3 0.0 copy-done
  1.3 0.0 copy-start.2
  1.3 0.0 copy-start.3
  1.3 0.0 copy-start.4
  1.3 0.0 copy-start.7
  1.3 0.0 copy-start.1
  1.3 0.0 copy-start.5
  1.3 0.7 %sort_rows.1 = bf16[1024,256]{1,0:T(8,128)(2,1)S(1)} custom-call(bf16[1024,1024]{1,0:T(8,128)(2,1)S(1)} %pick_rows.1.picks_ref, f32[1024,256]{1,0:T(8,128)S(1)} %copy-done), custom_call_target="tpu_custom_call" | custom-call | tf_op jit(solution)/shard_map/sort_rows/pallas_call | solution.py:119
  2.1 19.2 %all_to_all.5 = bf16[16,64,256]{2,1,0:T(8,128)(2,1)S(1)} all-to-all(bf16[16,64,256]{2,1,0:T(8,128)(2,1)S(1)} %bitcast.5), channel_id=1, replica_groups=mesh['grp'=8,'tm'=16] {'tm'}, dimensions={0} | all-to-all | bytes 1048576 | tf_op jit(solution)/shard_map/all_to_all | solution.py:279
  21.2 0.0 copy-done.2
  21.2 0.0 copy-done.3
  21.2 0.0 copy-done.4
  21.2 0.0 copy-done.7
  21.3 1.2 %whiten.1.refs_1_ = bf16[1024,128]{1,0:T(8,128)(2,1)S(1)} custom-call(bf16[1024,256]{1,0:T(8,128)(2,1)S(1)} %bitcast.6, bf16[512,256]{1,0:T(8,128)(2,1)S(1)} %copy-done.2, bf16[256,256]{1,0:T(8,128)(2,1)S(1)} %copy-done.3, bf16[128,128]{1,0:T(8,128)(2,1)S(1)} %copy-done.4, f32[8,128]{1,0:T(8,128)S(1)} %copy-done.7), custom_call_target="tpu_custom_call" | custom-call | tf_op jit(solution)/shard_map/whiten/pallas_call | solution.py:171
  22.4 0.6 %collective-permute-start.1 = (bf16[1024,128]{1,0:T(8,128)(2,1)S(1)}, bf16[1024,128]{1,0:T(8,128)(2,1)S(1)}, u32[]{:S(2)}, u32[]{:S(2)}) collective-permute-start(bf16[1024,128]{1,0:T(8,128)(2,1)S(1)} %whiten.1.refs_1_), channel_id=1, source_target_pairs={{0,1},{1,0},{2,3},{3,2},{4,5},{5,4},{6,7},{7,6},{8,9},{9,8},{10,11... | collective-permute-start | bytes 786440 | tf_op jit(solution)/shard_map/ppermute | solution.py:284
  23.1 1.9 %collective-permute-start = (bf16[1024,128]{1,0:T(8,128)(2,1)S(1)}, bf16[1024,128]{1,0:T(8,128)(2,1)S(1)}, u32[]{:S(2)}, u32[]{:S(2)}) collective-permute-start(bf16[1024,128]{1,0:T(8,128)(2,1)S(1)} %whiten.1.refs_1_), channel_id=1, source_target_pairs={{1,2},{2,1},{3,4},{4,3},{5,6},{6,5},{7,8},{8,7},{9,10},{10,9},{11,... | collective-permute-start | bytes 786440 | tf_op jit(solution)/shard_map/ppermute | solution.py:285
  25.0 4.1 %collective-permute-done.1.refs_2_ = bf16[1024,128]{1,0:T(8,128)(2,1)S(1)} collective-permute-done((bf16[1024,128]{1,0:T(8,128)(2,1)S(1)}, bf16[1024,128]{1,0:T(8,128)(2,1)S(1)}, u32[]{:S(2)}, u32[]{:S(2)}) %collective-permute-start.1) | collective-permute-done | bytes 262176 | tf_op jit(solution)/shard_map/ppermute | solution.py:284
  29.1 0.0 copy-done.1
  29.1 0.0 copy-done.5
  29.1 2.1 %correlate_0.1.refs_4_ = bf16[2,4096,128]{2,1,0:T(8,128)(2,1)} custom-call(s32[2,255]{1,0:T(2,128)S(1)} %bitcast.7, bf16[1024,128]{1,0:T(8,128)(2,1)S(1)} %whiten.1.refs_1_, bf16[1024,128]{1,0:T(8,128)(2,1)S(1)} %collective-permute-done.1.refs_2_, bf16[256,256]{1,0:T(8,128)(2,1)S(1)} %copy-done.1), custom_call_target="tpu_custom_call" | custom-call | tf_op jit(solution)/shard_map/correlate_0/pallas_call | solution.py:260
  31.2 4.4 %collective-permute-done.refs_2_ = bf16[1024,128]{1,0:T(8,128)(2,1)S(1)} collective-permute-done((bf16[1024,128]{1,0:T(8,128)(2,1)S(1)}, bf16[1024,128]{1,0:T(8,128)(2,1)S(1)}, u32[]{:S(2)}, u32[]{:S(2)}) %collective-permute-start) | collective-permute-done | bytes 262176 | tf_op jit(solution)/shard_map/ppermute | solution.py:285
  35.6 2.1 %correlate_1.1 = bf16[2,4096,128]{2,1,0:T(8,128)(2,1)} custom-call(s32[2,255]{1,0:T(2,128)S(1)} %bitcast.8, bf16[1024,128]{1,0:T(8,128)(2,1)S(1)} %whiten.1.refs_1_, bf16[1024,128]{1,0:T(8,128)(2,1)S(1)} %collective-permute-done.refs_2_, bf16[256,256]{1,0:T(8,128)(2,1)S(1)} %copy-done.1, ...), custom_call_target="tpu_custom_call", output_to_operand_aliasing={{}: (4, {})} | custom-call | tf_op jit(solution)/shard_map/correlate_1/pallas_call | solution.py:260
Async XLA Ops:
  0.0 1.3 %copy-start = (f32[1024,256]{1,0:T(8,128)S(1)}, f32[1024,256]{1,0:T(8,128)}, u32[]{:S(2)}) copy-start(f32[1024,256]{1,0:T(8,128)} %raw_ref.1) | copy-start | bytes 3145732
  0.0 0.8 %copy-start.6 = (s32[1,1024]{1,0:T(1,128)S(1)}, s32[1,1024]{1,0:T(1,128)}, u32[]{:S(2)}) copy-start(s32[1,1024]{1,0:T(1,128)} %param.11) | copy-start | bytes 12292
  1.3 20.0 %copy-start.2 = (bf16[512,256]{1,0:T(8,128)(2,1)S(1)}, bf16[512,256]{1,0:T(8,128)(2,1)}, u32[]{:S(2)}) copy-start(bf16[512,256]{1,0:T(8,128)(2,1)} %constant.10.clone.band_ref) | copy-start | bytes 786436
  1.3 20.0 %copy-start.3 = (bf16[256,256]{1,0:T(8,128)(2,1)S(1)}, bf16[256,256]{1,0:T(8,128)(2,1)}, u32[]{:S(2)}) copy-start(bf16[256,256]{1,0:T(8,128)(2,1)} %constant.11.clone.dft_ref) | copy-start | bytes 393220
  1.3 19.9 %copy-start.4 = (bf16[128,128]{1,0:T(8,128)(2,1)S(1)}, bf16[128,128]{1,0:T(8,128)(2,1)}, u32[]{:S(2)}) copy-start(bf16[128,128]{1,0:T(8,128)(2,1)} %constant.12.clone.smooth_ref) | copy-start | bytes 98308
  1.3 19.9 %copy-start.7 = (f32[8,128]{1,0:T(8,128)S(1)}, f32[8,128]{1,0:T(8,128)}, u32[]{:S(2)}) copy-start(f32[8,128]{1,0:T(8,128)} %constant.13.clone.scale_ref) | copy-start | bytes 12292
  1.3 27.8 %copy-start.1 = (bf16[256,256]{1,0:T(8,128)(2,1)S(1)}, bf16[256,256]{1,0:T(8,128)(2,1)}, u32[]{:S(2)}) copy-start(bf16[256,256]{1,0:T(8,128)(2,1)} %constant.14.clone.refs_3_) | copy-start | bytes 393220
  1.3 27.8 %copy-start.5 = (s32[255,2]{0,1:T(2,128)S(1)}, s32[255,2]{0,1:T(2,128)}, u32[]{:S(2)}) copy-start(s32[255,2]{0,1:T(2,128)} %param.12) | copy-start | bytes 6124
  22.4 6.7 %collective-permute-start.1 = (bf16[1024,128]{1,0:T(8,128)(2,1)S(1)}, bf16[1024,128]{1,0:T(8,128)(2,1)S(1)}, u32[]{:S(2)}, u32[]{:S(2)}) collective-permute-start(bf16[1024,128]{1,0:T(8,128)(2,1)S(1)} %whiten.1.refs_1_), channel_id=1, source_target_pairs={{0,1},{1,0},{2,3},{3,2},{4,5},{5,4},{6,7},{7,6},{8,9},{9,8},{10,11... | collective-permute-start | bytes 786440 | tf_op jit(solution)/shard_map/ppermute | solution.py:284
  23.1 12.5 %collective-permute-start = (bf16[1024,128]{1,0:T(8,128)(2,1)S(1)}, bf16[1024,128]{1,0:T(8,128)(2,1)S(1)}, u32[]{:S(2)}, u32[]{:S(2)}) collective-permute-start(bf16[1024,128]{1,0:T(8,128)(2,1)S(1)} %whiten.1.refs_1_), channel_id=1, source_target_pairs={{1,2},{2,1},{3,4},{4,3},{5,6},{6,5},{7,8},{8,7},{9,10},{10,9},{11,... | collective-permute-start | bytes 786440 | tf_op jit(solution)/shard_map/ppermute | solution.py:285
